TPU v7x, 128 devices: a whole 4x4x4 slice. The times are simulated.
128 devices in a mesh: wide: 16 (over x, y), narrow: 8 (over z, core).
Axes of the slice: x: 4, y: 4, z: 4, core: 2. Of those that a mesh axis runs over, the one named last changes fastest.
Arguments:
- tokens: bfloat16 [16384, 4608], P('wide', 'narrow'), may hold values from -6 to 6
- segment_ids: int32 [16384], P('wide'), may hold values from 0 to 7, never falling along the last dimension, each value on 1 to 8192 neighbouring positions
- page_table: int32 [128], P('wide'), may hold values from 0 to 127, as said below
- pre_gain: bfloat16 [4608], P('narrow'), may hold values from 0.099609375 to 1.8984375
- post_gain: bfloat16 [4608], P('narrow'), may hold values from 0.25 to 1.75
- w_query: bfloat16 [4608, 4096], P('wide', 'narrow'), may hold values from -0.25 to 0.25
- w_key: bfloat16 [4608, 2048], P('wide', 'narrow'), may hold values from -0.09375 to 0.09375
- w_value: bfloat16 [4608, 2048], P('wide', 'narrow'), may hold values from -0.09375 to 0.09375
- w_out: bfloat16 [4096, 4608], P('narrow', 'wide'), may hold values from -0.09375 to 0.09375
Outputs:
- mixed: bfloat16 [16384, 4608], P('wide', 'narrow')
- kv_pages: bfloat16 [128, 16, 128, 256], P('wide', 'narrow')
Inputs may be any that keep to these rules, and one draw needn't show every extreme that they name: page_table is a permutation; kv_pages places pages i * 8 to (i + 1) * 8 - 1 on wide index i; the 8 blocks of tokens held by one wide index go to pages placed on 8 different wide indices. `segment_ids`: segment ids never fall along the tokens; every prompt has at least one token and the longest has exactly 8192.
All inputs are finite; a program needn't handle non-finite values.
Results may differ from a plain program's by a relative error of at most 0.014.
Values may be sent and summed in bfloat16 or wider, within the bound.
A program may use at most 192 MiB of HBM per device.

v0:
```python
import functools
import math

import jax
import jax.numpy as jnp
from jax import lax
from jax.experimental import pallas as pl
from jax.experimental.pallas import tpu as pltpu
from jax.sharding import PartitionSpec as P

D = 4608
HD = 128
WINDOW = 4096
SEGS = 8

SOFT_CAP = 50.0
QUERY_SCALE = 1.0 / 12.0
NORM_EPSILON = 1e-06
NX, NY, NZ = 4, 4, 4
MESH = pl.DeviceIdType.MESH
PRE = QUERY_SCALE / SOFT_CAP
POST = SOFT_CAP * math.log2(math.e)


def shifted(value, axis, steps):
    count = lax.axis_size(axis)
    leading, last = (max(0, -steps), min(count, count - steps))
    return lax.ppermute(value, axis, [(source, source + steps) for source in range(leading, last)])


def rms_scale(values):
    return lax.rsqrt(jnp.mean(values * values, axis=-1, keepdims=True) + NORM_EPSILON)


def rotate_half(values, cosine, sine):
    half_width = values.shape[-1] // 2
    first_half = values[..., :half_width]
    second_half = values[..., half_width:]
    return jnp.concatenate(
        [first_half * cosine - second_half * sine, second_half * cosine + first_half * sine],
        axis=-1,
    )


def gather_kernel(
    tok_ref, w_ref, meta_ref, gain_ref,
    tok_all, w_all, meta_all, gain_all,
    w_send, w_recv, z_send, z_recv, c_send, c_recv, m_send, m_recv, g_send, g_recv, own_sem,
):
    wide = lax.axis_index("wide")
    narrow = lax.axis_index("narrow")
    x, y = lax.div(wide, NY), lax.rem(wide, NY)
    z, core = lax.div(narrow, 2), lax.rem(narrow, 2)
    shard = w_ref.shape[0]
    half = shard // 2
    cols = w_ref.shape[1] // 2
    rows = tok_ref.shape[0]

    def ring(position, count, step):
        return lax.rem(position + step + count, count)

    def at_wide(x_new, y_new):
        return {"wide": x_new * NY + y_new}

    def remote(src, dst, send, recv, where):
        return pltpu.make_async_remote_copy(
            src_ref=src, dst_ref=dst, send_sem=send, recv_sem=recv,
            device_id=where, device_id_type=MESH,
        )

    def peer(part, stage, step):
        if (part == 0) == (stage == 0):
            return at_wide(ring(x, NX, step), y)
        return at_wide(x, ring(y, NY, step))

    def block(part, along, across):
        if part == 0:
            return ring(x, NX, along) * NY + ring(y, NY, across)
        return ring(x, NX, across) * NY + ring(y, NY, along)

    def rows_of(part, along, across):
        return pl.ds(block(part, along, across) * shard + part * half, half)

    def send(part, group, kind, along, across, own=False):
        stage = 0 if group == 0 else 1
        where = peer(part, stage, 1 if kind % 2 == 0 else -1)
        there = rows_of(part, along, across)
        if kind < 2:
            span = slice(None)
        else:
            span = pl.ds((kind - 2) * cols, cols)
        if own:
            src = w_ref.at[pl.ds(part * half, half), span]
        else:
            src = w_all.at[there, span]
        return remote(
            src, w_all.at[there, span],
            w_send.at[part, group, kind], w_recv.at[part, group, kind], where,
        )

    started = []

    def start(copy):
        copy.start()
        started.append(copy)
        return copy

    sent = {}

    def go(part, group, kind, along, across, own=False):
        sent[part, group, kind] = start(send(part, group, kind, along, across, own))

    toks = {}

    def zgo(kind, index, src, span):
        where = {"narrow": ring(z, NZ, 1 if kind % 2 == 0 else -1) * 2 + core}
        toks[kind] = start(remote(src, tok_all.at[index, span], z_send.at[kind], z_recv.at[kind], where))

    pair = {}

    def cgo(kind, index, src, span):
        where = {"narrow": z * 2 + (1 - core)}
        pair[kind] = start(remote(src, tok_all.at[index, span], c_send.at[kind], c_recv.at[kind], where))

    every = pl.ds(0, rows)
    low, high = pl.ds(0, rows // 2), pl.ds(rows // 2, rows // 2)

    def zblock(step):
        return ring(z, NZ, step) * 2 + core

    small = []
    for other in range(1, NX * NY):
        target = lax.rem(wide + other, NX * NY)
        small.append(start(remote(
            meta_ref, meta_all.at[wide], m_send.at[other], m_recv.at[other], {"wide": target})))
    for other in range(1, NZ * 2):
        target = lax.rem(narrow + other, NZ * 2)
        small.append(start(remote(
            gain_ref, gain_all.at[narrow], g_send.at[other], g_recv.at[other], {"narrow": target})))

    for part in (0, 1):
        go(part, 0, 0, 0, 0, True)
        go(part, 0, 1, 0, 0, True)
    zgo(0, narrow, tok_ref, every)
    zgo(1, narrow, tok_ref, every)
    cgo(0, narrow, tok_ref, every)
    for part in (0, 1):
        go(part, 1, 0, 0, 0, True)
        go(part, 1, 1, 0, 0, True)
    local = [
        pltpu.make_async_copy(w_ref, w_all.at[pl.ds(wide * shard, shard)], own_sem.at[0]),
        pltpu.make_async_copy(tok_ref, tok_all.at[narrow], own_sem.at[1]),
        pltpu.make_async_copy(meta_ref, meta_all.at[wide], own_sem.at[2]),
        pltpu.make_async_copy(gain_ref, gain_all.at[narrow], own_sem.at[3]),
    ]
    for copy in local:
        copy.start()

    for part in (0, 1):
        sent[part, 0, 0].wait_recv()
        go(part, 0, 2, -1, 0)
        go(part, 2, 0, -1, 0)
        go(part, 2, 1, -1, 0)
    for part in (0, 1):
        sent[part, 0, 1].wait_recv()
        go(part, 0, 3, 1, 0)
        go(part, 3, 0, 1, 0)
        go(part, 3, 1, 1, 0)

    toks[0].wait_recv()
    zgo(2, zblock(-1), tok_all.at[zblock(-1), low], low)
    cgo(1, zblock(-1), tok_all.at[zblock(-1)], every)
    toks[1].wait_recv()
    zgo(3, zblock(1), tok_all.at[zblock(1), high], high)
    cgo(2, zblock(1), tok_all.at[zblock(1)], every)

    for part in (0, 1):
        sent[part, 1, 0].wait_recv()
        go(part, 1, 2, 0, -1)
        sent[part, 1, 1].wait_recv()
        go(part, 1, 3, 0, 1)
    for part in (0, 1):
        sent[part, 0, 2].wait_recv()
        sent[part, 0, 3].wait_recv()
        go(part, 4, 0, 2, 0)
        go(part, 4, 1, 2, 0)
    for group, along in ((2, -1), (3, 1)):
        for part in (0, 1):
            sent[part, group, 0].wait_recv()
            go(part, group, 2, along, -1)
            sent[part, group, 1].wait_recv()
            go(part, group, 3, along, 1)
    toks[2].wait_recv()
    cgo(3, zblock(2), tok_all.at[zblock(2), low], low)
    toks[3].wait_recv()
    cgo(4, zblock(2), tok_all.at[zblock(2), high], high)
    for part in (0, 1):
        sent[part, 4, 0].wait_recv()
        go(part, 4, 2, 2, -1)
        sent[part, 4, 1].wait_recv()
        go(part, 4, 3, 2, 1)

    for part in (0, 1):
        for group in range(1, 5):
            sent[part, group, 2].wait_recv()
            sent[part, group, 3].wait_recv()
    for kind in range(5):
        pair[kind].wait_recv()
    for copy in small:
        copy.wait_recv()
    for copy in local:
        copy.wait()
    for copy in started:
        copy.wait_send()


def gather_all(tokens, weights, meta, gain):
    rows, width = tokens.shape
    shard, columns = weights.shape
    any_spec = pl.BlockSpec(memory_space=pl.ANY)
    vmem_spec = pl.BlockSpec(memory_space=pltpu.VMEM)
    dma = pltpu.SemaphoreType.DMA
    return pl.pallas_call(
        gather_kernel,
        out_shape=(
            jax.ShapeDtypeStruct((8, rows, width), tokens.dtype),
            jax.ShapeDtypeStruct((16 * shard, columns), weights.dtype),
            jax.ShapeDtypeStruct((16,) + meta.shape, meta.dtype),
            jax.ShapeDtypeStruct((8,) + gain.shape, gain.dtype),
        ),
        in_specs=[vmem_spec] * 4,
        out_specs=(any_spec,) * 4,
        scratch_shapes=[
            dma((2, 5, 4)), dma((2, 5, 4)), dma((4,)), dma((4,)), dma((5,)), dma((5,)),
            dma((16,)), dma((16,)), dma((8,)), dma((8,)), dma((4,)),
        ],
        compiler_params=pltpu.CompilerParams(has_side_effects=True),
        name="gather_all",
    )(tokens, weights, meta, gain)


QB = 256


def attention_kernel(q_ref, floor_ref, k0, k1, k2, k3, k4, out_ref, held, total, sems):
    sources = (k0, k1, k2, k3, k4)
    tokens = q_ref.shape[0]
    blocks = tokens // QB
    copies = [
        pltpu.make_async_copy(source, held.at[d], sems.at[d]) for d, source in enumerate(sources)
    ]
    for copy in copies:
        copy.start()

    def lanes(start, size):
        return pl.ds(pl.multiple_of(start, 128), size)

    def chunk(d, g, qb, first, size, diagonal=False, fresh=False):
        qrows = pl.ds(pl.multiple_of(qb * QB, QB), QB)
        krows = pl.ds(pl.multiple_of(first, 256), size)
        query = jnp.concatenate(
            [q_ref[qrows, lanes(g * 256, 128)], q_ref[qrows, lanes(g * 256 + 128, 128)]], axis=0
        )
        keys = held[d, krows, lanes(g * 256, 128)]
        values = held[d, krows, lanes(g * 256 + 128, 128)]
        scores = lax.dot_general(
            query, keys, (((1,), (1,)), ((), ())), preferred_element_type=jnp.float32
        )
        floor = floor_ref[qrows, :] - ((4 - d) * tokens + first)
        floor = jnp.concatenate([floor] * (size // 128), axis=1)
        column = lax.broadcasted_iota(jnp.int32, (QB, size), 1)
        allowed = column >= floor
        if diagonal:
            allowed = allowed & (column <= lax.broadcasted_iota(jnp.int32, (QB, size), 0))
        weights = jnp.exp2(jnp.tanh(scores * PRE) * POST)
        weights = jnp.concatenate(
            [
                jnp.where(allowed, weights[:QB], 0.0).astype(jnp.bfloat16),
                jnp.where(allowed, weights[QB:], 0.0).astype(jnp.bfloat16),
            ],
            axis=0,
        )
        wide_values = jnp.concatenate([values, jnp.ones_like(values)], axis=1)
        product = jnp.dot(weights, wide_values, preferred_element_type=jnp.float32)
        slot = g * blocks + qb
        if fresh:
            total[slot] = product
        else:
            total[slot] += product

    for d in range(5):
        copies[d].wait()

        def pair(t, carry):
            g, qb = lax.div(t, blocks), lax.rem(t, blocks)
            if d == 0:
                chunk(0, g, qb, qb * QB, QB, diagonal=True, fresh=True)
                lax.fori_loop(0, qb, lambda k, c: (chunk(0, g, qb, k * QB, QB), c)[1], 0)
            elif d < 4:
                chunk(d, g, qb, 0, tokens // 2)
                chunk(d, g, qb, tokens // 2, tokens // 2)
            else:
                lax.fori_loop(qb, blocks, lambda k, c: (chunk(4, g, qb, k * QB, QB), c)[1], 0)
                slot = g * blocks + qb
                result = (total[slot, :, :HD] / total[slot, :, HD:]).astype(out_ref.dtype)
                qrows = pl.ds(pl.multiple_of(qb * QB, QB), QB)
                out_ref[qrows, lanes(g * 256, 128)] = result[:QB]
                out_ref[qrows, lanes(g * 256 + 128, 128)] = result[QB:]
            return carry

        lax.fori_loop(0, 2 * blocks, pair, 0)


def attention(query, floor, sources):
    tokens = query.shape[0]
    vmem_spec = pl.BlockSpec(memory_space=pltpu.VMEM)
    any_spec = pl.BlockSpec(memory_space=pl.ANY)
    return pl.pallas_call(
        attention_kernel,
        out_shape=jax.ShapeDtypeStruct(query.shape, jnp.bfloat16),
        in_specs=[vmem_spec, vmem_spec] + [any_spec] * 5,
        out_specs=vmem_spec,
        scratch_shapes=[
            pltpu.VMEM((5,) + sources[0].shape, jnp.bfloat16),
            pltpu.VMEM((8, 2 * QB, 256), jnp.float32),
            pltpu.SemaphoreType.DMA((5,)),
        ],
        cost_estimate=pl.CostEstimate(
            flops=4 * tokens * 4352 * 128 * 8, bytes_accessed=8 << 20,
            transcendentals=8 * tokens * 4352,
        ),
        compiler_params=pltpu.CompilerParams(vmem_limit_bytes=40 << 20),
        name="attention",
    )(query, floor, *sources)


def local(tokens, segment_ids, page_table, pre_gain, post_gain, w_query, w_key, w_value, w_out):
    tok_w = tokens.shape[0]
    shard_count = lax.axis_size("wide")
    shard_index = lax.axis_index("wide")
    block_count = page_table.shape[0]
    seg_rows = segment_ids.reshape(8, tok_w // 8)
    table_row = jnp.pad(page_table[None, :], ((0, 7), (0, tok_w // 8 - block_count)))
    meta = jnp.concatenate([seg_rows, table_row], axis=0)
    gain_in = jnp.pad(pre_gain[None, :], ((0, 15), (0, 64)))
    weights = jnp.concatenate([w_query, w_key, w_value], axis=1)
    tok_all, w_all, meta_all, gain_all = gather_all(tokens, weights, meta, gain_in)

    residual = tokens.astype(jnp.float32)
    gathered = jnp.transpose(tok_all, (1, 0, 2)).reshape(tok_w, D)
    features = gathered.astype(jnp.float32)
    gain = gain_all[:, 0, : pre_gain.shape[0]].reshape(D)
    normed = (features * rms_scale(features) * gain.astype(jnp.float32)).astype(jnp.bfloat16)

    labels = jnp.arange(SEGS, dtype=jnp.int32)
    all_ids = meta_all[:, :8, :].reshape(-1)
    table_all = meta_all[:, 8, :block_count].reshape(-1)
    seg_firsts = jnp.sum((all_ids[:, None] < labels[None, :]).astype(jnp.int32), axis=0)
    member = segment_ids[:, None] == labels[None, :]
    seg_start = jnp.sum(jnp.where(member, seg_firsts[None, :], 0), axis=1)
    first_token = shard_index * tok_w
    token_index = first_token + jnp.arange(tok_w, dtype=jnp.int32)
    positions = token_index - seg_start
    half_width = HD // 2
    inverse_freq = jnp.exp(
        -math.log(10000.0) * 2.0 * jnp.arange(half_width, dtype=jnp.float32) / HD
    )
    angle_table = positions.astype(jnp.float32)[:, None] * inverse_freq[None, :]
    cosine = jnp.cos(angle_table)[:, None, :]
    sine = jnp.sin(angle_table)[:, None, :]

    heads_here = w_query.shape[1] // HD
    pairs_here = w_key.shape[1] // HD
    raw = jnp.dot(normed, w_all, preferred_element_type=jnp.float32)
    q_width, k_width = w_query.shape[1], w_key.shape[1]
    query_raw = raw[:, :q_width]
    key_raw = raw[:, q_width : q_width + k_width]
    value_raw = raw[:, q_width + k_width :]
    keys_new = rotate_half(key_raw.reshape(tok_w, pairs_here, HD), cosine, sine).astype(
        jnp.bfloat16
    )
    values_new = value_raw.reshape(tok_w, pairs_here, HD).astype(jnp.bfloat16)
    paired = jnp.concatenate([keys_new, values_new], axis=2)
    flat = paired.reshape(tok_w, pairs_here * 2 * HD)
    reach_depth = min((WINDOW - 1) // tok_w + 1, shard_count - 1)
    sources = [flat] + [shifted(flat, "wide", distance + 1) for distance in range(reach_depth)]
    query_new = rotate_half(query_raw.reshape(tok_w, heads_here, HD), cosine, sine).astype(
        jnp.bfloat16
    ).reshape(tok_w, heads_here * HD)
    key_floor = jnp.maximum(seg_start, token_index - WINDOW + 1) - (first_token - WINDOW)
    floor = jnp.broadcast_to(key_floor[:, None], (tok_w, 128))
    w_out_late, _ = lax.optimization_barrier((w_out, w_all[:8, :128]))
    w_out_all = lax.all_gather(w_out_late, "wide", axis=1, tiled=True)
    attn_out = attention(query_new, floor, sources)

    head_terms = jnp.dot(attn_out, w_out_all, preferred_element_type=jnp.float32)
    projected = lax.psum_scatter(
        head_terms.astype(jnp.bfloat16), "narrow", scatter_dimension=1, tiled=True
    ).astype(jnp.float32)
    square_sums = lax.psum(jnp.sum(projected * projected, axis=1), "narrow")
    post_scale = lax.rsqrt(square_sums / D + NORM_EPSILON)
    mixed = (residual + projected * post_scale[:, None] * post_gain.astype(jnp.float32)).astype(
        jnp.bfloat16
    )
    page_len = tok_w // block_count
    token_blocks = paired.reshape(block_count, page_len, pairs_here, 2 * HD)
    owners = page_table // block_count
    shard_ids = jnp.arange(shard_count, dtype=jnp.int32)
    send_pick = (owners[None, :] == shard_ids[:, None]).astype(jnp.bfloat16)
    outgoing = jnp.einsum(
        "sj,jpgc->sgpc", send_pick, token_blocks, preferred_element_type=jnp.float32
    ).astype(jnp.bfloat16)
    incoming = lax.all_to_all(outgoing, "wide", split_axis=0, concat_axis=0, tiled=True)
    my_pages = shard_index * block_count + jnp.arange(block_count, dtype=jnp.int32)
    found_page = table_all[None, :] == my_pages[:, None]
    anchor = jnp.sum(
        jnp.where(
            found_page, jnp.arange(table_all.shape[0], dtype=jnp.int32)[None, :] // block_count, 0
        ),
        axis=1,
    )
    take_pick = (anchor[:, None] == shard_ids[None, :]).astype(jnp.bfloat16)
    kv_pages = jnp.einsum(
        "qs,sgpc->qgpc", take_pick, incoming, preferred_element_type=jnp.float32
    ).astype(jnp.bfloat16)
    return (mixed, kv_pages)


def solution(mesh):
    return jax.shard_map(
        local,
        mesh=mesh,
        in_specs=(
            P("wide", "narrow"),
            P("wide"),
            P("wide"),
            P("narrow"),
            P("narrow"),
            P("wide", "narrow"),
            P("wide", "narrow"),
            P("wide", "narrow"),
            P("narrow", "wide"),
        ),
        out_specs=(P("wide", "narrow"), P("wide", "narrow", None, None)),
        check_vma=False,
    )
```

profile of v0, /device:TPU:1, one launch (start us, length us, event | category | flops | bytes accessed | tf_op | source)
XLA Modules:
  0.0 395.8 jit_solution(15772181968869966171)
XLA Ops:
  8.7 2.4 copy.56.tok_ref
  13.2 88.3 %gather_all.1 = (bf16[8,1024,576]{2,1,0:T(8,128)(2,1)}, bf16[4608,1024]{1,0:T(8,128)(2,1)}, s32[16,16,128]{2,1,0:T(8,128)}, bf16[8,16,640]{2,1,0:T(8,128)(2,1)}) custom-call(bf16[1024,576]{1,0:T(8,128)(2,1)} %copy.56.tok_ref, bf16[288,1024]{1,0:T(8,128)(2,1)} %pad_maximum_fusion.2.w_ref, s32[16,128]{1,0:T(8,128)} %pad_add_fusion.meta_ref, ...), custom_call_target="tpu_custom_call" | custom-call | tf_op jit(solution)/shard_map/gather_all/pallas_call | solution.py:223
  101.6 6.2 %fusion = f32[1024]{0:T(1024)S(1)} fusion(bf16[8,1024,576]{2,1,0:T(8,128)(2,1)} %get-tuple-element.6), kind=kLoop, calls=%fused_computation.2 | loop fusion | flops 14154752 | bytes 9441280 | tf_op jit(solution)/shard_map/reduce_sum | solution.py:32
  107.8 12.3 %convert_bitcast_fusion = f32[1024,8,576]{2,0,1:T(8,128)} fusion(bf16[8,1024,576]{2,1,0:T(8,128)(2,1)} %get-tuple-element.6), kind=kLoop, calls=%fused_computation.1 | loop fusion | flops 4718592 | bytes 28311552 | tf_op jit(solution)/shard_map/convert_element_type | solution.py:351
  121.1 22.1 %copy.57 = f32[1024,8,576]{0,2,1:T(8,128)} copy(f32[1024,8,576]{2,0,1:T(8,128)} %convert_bitcast_fusion) | data formatting | bytes 37748736 | tf_op jit(solution)/shard_map/convert_element_type | solution.py:351
  143.3 8.1 %fusion.2 = bf16[1024,4608]{0,1:T(8,128)(2,1)S(1)} fusion(f32[1024,8,576]{0,2,1:T(8,128)} %copy.57, f32[4608]{0:T(1024)S(1)} %reshape.169, f32[1024]{0:T(1024)S(1)} %add_rsqrt_fusion.1), kind=kLoop, calls=%fused_computation.5 | loop fusion | flops 14155776 | bytes 28334080 | tf_op jit(solution)/shard_map/convert_element_type | solution.py:353
  151.4 12.7 %fusion.25 = f32[1024,1024]{0,1:T(8,128)S(1)} fusion(bf16[1024,4608]{0,1:T(8,128)(2,1)S(1)} %fusion.2, bf16[4608,1024]{1,0:T(8,128)(2,1)} %get-tuple-element.8), kind=kOutput, calls=%fused_computation.66 | convolution fusion | flops 9663676416 | bytes 23068672 | tf_op jit(solution)/shard_map/dot_general | solution.py:374
  169.1 2.4 pad_maximum_fusion.1
  171.8 3.3 collective-permute-start.3
  175.0 2.9 collective-permute-start.2
  178.0 4.6 %collective-permute-start.1 = (bf16[1024,512]{1,0:T(8,128)(2,1)S(1)}, bf16[1024,512]{1,0:T(8,128)(2,1)}, u32[]{:S(2)}, u32[]{:S(2)}) collective-permute-start(bf16[1024,512]{1,0:T(8,128)(2,1)S(1)} %bitcast.55), channel_id=1, source_target_pairs={{0,16},{8,24},{16,32},{24,40},{32,48},{40,56},{48,64},{56,72},{64,... | collective-permute-start | bytes 3145736 | tf_op jit(solution)/shard_map/ppermute | solution.py:28
  182.5 3.2 collective-permute-start
  191.7 2.8 copy.73
  194.5 2.7 copy.72
  197.2 3.0 subtract_convert_fusion
  201.9 19.8 %collective-permute-done.2.k3 = bf16[1024,512]{1,0:T(8,128)(2,1)S(1)} collective-permute-done((bf16[1024,512]{1,0:T(8,128)(2,1)S(1)}, bf16[1024,512]{1,0:T(8,128)(2,1)S(1)}, u32[]{:S(2)}, u32[]{:S(2)}) %collective-permute-start.2) | collective-permute-done | bytes 1048608 | tf_op jit(solution)/shard_map/ppermute | solution.py:28
  221.7 3.5 collective-permute-done.k1
  225.4 37.7 %attention.1 = bf16[1024,512]{1,0:T(8,128)(2,1)S(1)} custom-call(bf16[1024,512]{1,0:T(8,128)(2,1)S(1)} %bitcast.58, s32[1024,128]{1,0:T(8,128)S(1)} %broadcast_in_dim.30.floor_ref, bf16[1024,512]{1,0:T(8,128)(2,1)S(1)} %bitcast.57, bf16[1024,512]{1,0:T(8,128)(2,1)} %collective-permute-done.k1, bf16[1024,512]{1,0:T(8,128)(2,1)} %collective-permute-done.1.k2, ...), custom_call_target="tpu_custom_call" | custom-call | flops 18253611008 | bytes 8388608 | tf_op jit(solution)/shard_map/attention/pallas_call | solution.py:318
  264.1 9.4 %convolution_convert_fusion = bf16[1024,4608]{0,1:T(8,128)(2,1)} fusion(bf16[1024,512]{1,0:T(8,128)(2,1)} %copy-done, bf16[512,4608]{0,1:T(8,128)(2,1)} %all-gather.2.cloned.1.call-done), kind=kOutput, calls=%fused_computation.6 | convolution fusion | flops 4836556800 | bytes 15204352 | tf_op jit(solution)/shard_map/dot_general | solution.py:396
  279.2 45.2 %all-to-all-start = ((bf16[16,2,128,256]{3,2,1,0:T(8,128)(2,1)}), bf16[16,2,128,256]{3,2,1,0:T(8,128)(2,1)S(1)}, u32[]{:S(2)}, u32[]{:S(2)}) async-start(bf16[16,2,128,256]{3,2,1,0:T(8,128)(2,1)} %copy.68), calls=%async_computation.1 | async-start | bytes 4194304 | tf_op jit(solution)/shard_map/all_to_all | solution.py:413
  324.7 25.2 %all-to-all-done = bf16[16,2,128,256]{3,2,1,0:T(8,128)(2,1)S(1)} async-done(((bf16[16,2,128,256]{3,2,1,0:T(8,128)(2,1)}), bf16[16,2,128,256]{3,2,1,0:T(8,128)(2,1)S(1)}, u32[]{:S(2)}, u32[]{:S(2)}) %all-to-all-start) | async-done | bytes 2097184 | tf_op jit(solution)/shard_map/all_to_all | solution.py:413
  352.4 19.2 %reduce-scatter.2.cloned.1.call-done = bf16[1024,576]{0,1:T(8,128)(2,1)} async-done(((bf16[1024,4608]{0,1:T(8,128)(2,1)}), bf16[1024,576]{0,1:T(8,128)(2,1)}) %reduce-scatter.2.cloned.1.call-update) | async-done | bytes 1179664 | tf_op jit(solution)/shard_map/reduce_scatter | solution.py:397
  373.1 13.2 %psum.7 = f32[1024]{0:T(1024)S(1)} all-reduce(f32[1024]{0:T(1024)S(1)} %fusion.3), channel_id=1, replica_groups=mesh['wide'=16,'narrow'=8] {'narrow'}, use_global_device_ids=true, to_apply=%region_5.6 | all-reduce | flops 1024 | bytes 8192 | tf_op jit(solution)/shard_map/psum | solution.py:400
  386.3 2.7 fusion.6
  (85 shorter events, 28.4 us)
Async XLA Ops:
  7.2 3.9 copy-start.12
  7.2 3.9 copy-start.14
  7.2 5.1 %copy-start.9 = (bf16[288,256]{1,0:T(8,128)(2,1)S(1)}, bf16[288,256]{1,0:T(8,128)(2,1)}, u32[]{:S(2)}) copy-start(bf16[288,256]{1,0:T(8,128)(2,1)} %param.16) | copy-start | bytes 442372
  7.2 5.1 %copy-start.10 = (bf16[288,256]{1,0:T(8,128)(2,1)S(1)}, bf16[288,256]{1,0:T(8,128)(2,1)}, u32[]{:S(2)}) copy-start(bf16[288,256]{1,0:T(8,128)(2,1)} %param.15) | copy-start | bytes 442372
  7.2 5.1 %copy-start.8 = (bf16[288,512]{1,0:T(8,128)(2,1)S(1)}, bf16[288,512]{1,0:T(8,128)(2,1)}, u32[]{:S(2)}) copy-start(bf16[288,512]{1,0:T(8,128)(2,1)} %param.14) | copy-start | bytes 884740
  7.2 256.9 %all-gather.2.cloned.1.call-start = ((), (), s32[]{:S(2)}) async-start(), calls=%async_computation.2 | async-start | bytes 5013504 | tf_op jit(solution)/shard_map/all_gather | solution.py:393
  8.0 363.6 %reduce-scatter.2.cloned.1.call-start = ((), (), s32[]{:S(2)}) async-start(), calls=%async_computation.3 | async-start | bytes 10616832 | tf_op jit(solution)/shard_map/reduce_scatter | solution.py:397
  164.1 2.1 copy-start.1
  164.1 2.6 copy-start.11
  168.1 3.4 copy-start.3
  168.3 3.2 copy-start.4
  168.3 3.2 copy-start.6
  171.8 30.1 %collective-permute-start.3 = (bf16[1024,512]{1,0:T(8,128)(2,1)S(1)}, bf16[1024,512]{1,0:T(8,128)(2,1)S(1)}, u32[]{:S(2)}, u32[]{:S(2)}) collective-permute-start(bf16[1024,512]{1,0:T(8,128)(2,1)S(1)} %bitcast.53), channel_id=1, source_target_pairs={{0,32},{8,40},{16,48},{24,56},{32,64},{40,72},{48,80},{56,88},{64,... | collective-permute-start | bytes 3145736 | tf_op jit(solution)/shard_map/ppermute | solution.py:28
  175.0 46.6 %collective-permute-start.2 = (bf16[1024,512]{1,0:T(8,128)(2,1)S(1)}, bf16[1024,512]{1,0:T(8,128)(2,1)S(1)}, u32[]{:S(2)}, u32[]{:S(2)}) collective-permute-start(bf16[1024,512]{1,0:T(8,128)(2,1)S(1)} %bitcast.54), channel_id=1, source_target_pairs={{0,24},{8,32},{16,40},{24,48},{32,56},{40,64},{48,72},{56,80},{64,... | collective-permute-start | bytes 3145736 | tf_op jit(solution)/shard_map/ppermute | solution.py:28
  178.0 43.7 %collective-permute-start.1 = (bf16[1024,512]{1,0:T(8,128)(2,1)S(1)}, bf16[1024,512]{1,0:T(8,128)(2,1)}, u32[]{:S(2)}, u32[]{:S(2)}) collective-permute-start(bf16[1024,512]{1,0:T(8,128)(2,1)S(1)} %bitcast.55), channel_id=1, source_target_pairs={{0,16},{8,24},{16,32},{24,40},{32,48},{40,56},{48,64},{56,72},{64,... | collective-permute-start | bytes 3145736 | tf_op jit(solution)/shard_map/ppermute | solution.py:28
  182.5 42.7 %collective-permute-start = (bf16[1024,512]{1,0:T(8,128)(2,1)S(1)}, bf16[1024,512]{1,0:T(8,128)(2,1)}, u32[]{:S(2)}, u32[]{:S(2)}) collective-permute-start(bf16[1024,512]{1,0:T(8,128)(2,1)S(1)} %bitcast.56), channel_id=1, source_target_pairs={{0,8},{8,16},{16,24},{24,32},{32,40},{40,48},{48,56},{56,64},{64,7... | collective-permute-start | bytes 3145736 | tf_op jit(solution)/shard_map/ppermute | solution.py:28
  188.7 1.6 slice-start
  263.1 1.0 copy-start
  273.5 1.9 copy-start.7
  273.5 2.3 copy-start.5
  279.2 45.2 %copy-start.13 = (bf16[576]{0:T(1024)(128)(2,1)S(1)}, bf16[576]{0:T(1024)(128)(2,1)}, u32[]{:S(2)}) copy-start(bf16[576]{0:T(1024)(128)(2,1)} %param.13) | copy-start | bytes 3460
  279.2 70.7 %all-to-all-start = ((bf16[16,2,128,256]{3,2,1,0:T(8,128)(2,1)}), bf16[16,2,128,256]{3,2,1,0:T(8,128)(2,1)S(1)}, u32[]{:S(2)}, u32[]{:S(2)}) async-start(bf16[16,2,128,256]{3,2,1,0:T(8,128)(2,1)} %copy.68), calls=%async_computation.1 | async-start | bytes 4194304 | tf_op jit(solution)/shard_map/all_to_all | solution.py:413
  351.2 35.1 %copy-start.2 = (bf16[1024,576]{0,1:T(8,128)(2,1)S(1)}, bf16[1024,576]{0,1:T(8,128)(2,1)}, u32[]{:S(2)}) copy-start(bf16[1024,576]{0,1:T(8,128)(2,1)} %param.9) | copy-start | bytes 3538948
Sparse Core Ops, SparseCore 0:
  10.2 78.4 all-gather.1
  273.6 97.8 reduce-scatter.1
where the time goes:
time: 397 us; the launch traced here: 396 us
  Pallas kernels  126 us (32%)
  waiting for transfers between devices  68.5 us (17%)
  starting transfers between devices  59.2 us (15%)
  local copies, waits for them, and re-layouts  48.4 us (12%)
  other arithmetic  41.9 us (11%)
  matrix products  24.2 us (6%)
  between operations  14.5 us (4%)
  blocking collectives  13.2 us (3%)
    pallas_call x1, Pallas kernels, gather_all(): pl.pallas_call(gather_kernel, out_shape=(jax.ShapeDtypeStruct((8, rows, w...  88.3 us
    all_to_all x1, starting transfers between devices, local(): lax.all_to_all(outgoing, 'wide', split_axis=0, concat_axis=0, tiled=True)  45.2 us
    pallas_call x1, Pallas kernels, attention(): pl.pallas_call(attention_kernel, out_shape=jax.ShapeDtypeStruct(query.sha...  37.7 us
    all_to_all x1, waiting for transfers between devices, local(): lax.all_to_all(outgoing, 'wide', split_axis=0, concat_axis=0, tiled=True)  25.2 us
    ppermute x4, waiting for transfers between devices, shifted(): lax.ppermute(value, axis, [(source, source + steps) for source in range(l...  23.3 us
    convert_element_type x1, local copies, waits for them, and re-layouts, local(): features = gathered.astype(jnp.float32)  22.1 us
    reduce_scatter x1, waiting for transfers between devices, local(): lax.psum_scatter(head_terms.astype(jnp.bfloat16), 'narrow', scatter_dimen...  19.2 us
    unnamed x40, local copies, waits for them, and re-layouts  14 us
  transfers between devices with their start and end apart: 7, of which 4 were waited for; matrix products, arithmetic and copies ran while one was open for 24% of the time, Pallas kernels for 32%

commit v1 on v0

--- a/solution.py
+++ b/solution.py
@@ -20,26 +20,6 @@
 MESH = pl.DeviceIdType.MESH
 PRE = QUERY_SCALE / SOFT_CAP
 POST = SOFT_CAP * math.log2(math.e)
-
-
-def shifted(value, axis, steps):
-    count = lax.axis_size(axis)
-    leading, last = (max(0, -steps), min(count, count - steps))
-    return lax.ppermute(value, axis, [(source, source + steps) for source in range(leading, last)])
-
-
-def rms_scale(values):
-    return lax.rsqrt(jnp.mean(values * values, axis=-1, keepdims=True) + NORM_EPSILON)
-
-
-def rotate_half(values, cosine, sine):
-    half_width = values.shape[-1] // 2
-    first_half = values[..., :half_width]
-    second_half = values[..., half_width:]
-    return jnp.concatenate(
-        [first_half * cosine - second_half * sine, second_half * cosine + first_half * sine],
-        axis=-1,
-    )
 
 
 def gather_kernel(
@@ -240,33 +220,113 @@
 
 
 QB = 256
-
-
-def attention_kernel(q_ref, floor_ref, k0, k1, k2, k3, k4, out_ref, held, total, sems):
-    sources = (k0, k1, k2, k3, k4)
-    tokens = q_ref.shape[0]
+REACH = 4
+
+
+def lanes(start, size):
+    return pl.ds(pl.multiple_of(start, 128), size)
+
+
+def attention_kernel(
+    tok_hbm, w_hbm, gain_ref, cos_ref, sin_ref, floor_ref,
+    out_ref, kv_hbm,
+    tok, w, query_all, held, total, tok_sem, w_sem, kv_sem, send, recv,
+):
+    parts, tokens, width = tok.shape
     blocks = tokens // QB
-    copies = [
-        pltpu.make_async_copy(source, held.at[d], sems.at[d]) for d, source in enumerate(sources)
+    half = w.shape[1] // 2
+    wide = lax.axis_index("wide")
+    count = NX * NY
+
+    def block_rows(b):
+        return pl.ds(pl.multiple_of(b * QB, QB), QB)
+
+    def load_tok(b):
+        return pltpu.make_async_copy(
+            tok_hbm.at[:, block_rows(b), :], tok.at[:, block_rows(b), :], tok_sem.at[b]
+        )
+
+    loads_w = [
+        pltpu.make_async_copy(
+            w_hbm.at[:, pl.ds(part * half, half)], w.at[:, pl.ds(part * half, half)], w_sem.at[part]
+        )
+        for part in range(2)
     ]
-    for copy in copies:
-        copy.start()
-
-    def lanes(start, size):
-        return pl.ds(pl.multiple_of(start, 128), size)
+    load_tok(0).start()
+    loads_w[0].start()
+    for b in range(1, blocks):
+        load_tok(b).start()
+    loads_w[1].start()
+
+    def rotated(value, rows):
+        return value * cos_ref[rows, :] + pltpu.roll(value, HD // 2, 1) * sin_ref[rows, :]
+
+    loads_w[0].wait()
+
+    def key_block(b, carry):
+        load_tok(b).wait()
+        rows = block_rows(b)
+        squares = jnp.zeros((QB, 1), jnp.float32)
+        for n in range(parts):
+            piece = tok[n, rows, :].astype(jnp.float32)
+            squares += jnp.sum(piece * piece, axis=1, keepdims=True)
+        scale = lax.rsqrt(squares / D + NORM_EPSILON)
+        product = jnp.zeros((QB, half), jnp.float32)
+        for n in range(parts):
+            piece = tok[n, rows, :].astype(jnp.float32)
+            normed = (piece * scale * gain_ref[n, 0:1, :].astype(jnp.float32)).astype(jnp.bfloat16)
+            tok[n, rows, :] = normed
+            product += jnp.dot(
+                normed, w[pl.ds(n * width, width), 0:half], preferred_element_type=jnp.float32
+            )
+        for g in range(2):
+            key = product[:, g * 256 : g * 256 + HD]
+            held[0, rows, g * 256 : g * 256 + HD] = rotated(key, rows).astype(jnp.bfloat16)
+            held[0, rows, g * 256 + HD : g * 256 + 256] = product[
+                :, g * 256 + HD : g * 256 + 256
+            ].astype(jnp.bfloat16)
+        return carry
+
+    lax.fori_loop(0, blocks, key_block, 0)
+    save = pltpu.make_async_copy(held.at[0], kv_hbm, kv_sem)
+    save.start()
+    moves = {}
+    for d in (1, 4, 2, 3):
+        moves[d] = pltpu.make_async_remote_copy(
+            src_ref=held.at[0], dst_ref=held.at[d], send_sem=send.at[d], recv_sem=recv.at[d],
+            device_id={"wide": lax.rem(wide + d, count)}, device_id_type=MESH,
+        )
+        moves[d].start()
+    loads_w[1].wait()
+
+    def query_block(b, carry):
+        rows = block_rows(b)
+        product = jnp.zeros((QB, half), jnp.float32)
+        for n in range(parts):
+            product += jnp.dot(
+                tok[n, rows, :], w[pl.ds(n * width, width), half : 2 * half],
+                preferred_element_type=jnp.float32,
+            )
+        for h in range(half // HD):
+            value = product[:, h * HD : (h + 1) * HD]
+            query_all[rows, h * HD : (h + 1) * HD] = rotated(value, rows).astype(jnp.bfloat16)
+        return carry
+
+    lax.fori_loop(0, blocks, query_block, 0)
 
     def chunk(d, g, qb, first, size, diagonal=False, fresh=False):
-        qrows = pl.ds(pl.multiple_of(qb * QB, QB), QB)
+        qrows = block_rows(qb)
         krows = pl.ds(pl.multiple_of(first, 256), size)
         query = jnp.concatenate(
-            [q_ref[qrows, lanes(g * 256, 128)], q_ref[qrows, lanes(g * 256 + 128, 128)]], axis=0
+            [query_all[qrows, lanes(g * 256, 128)], query_all[qrows, lanes(g * 256 + 128, 128)]],
+            axis=0,
         )
         keys = held[d, krows, lanes(g * 256, 128)]
         values = held[d, krows, lanes(g * 256 + 128, 128)]
         scores = lax.dot_general(
             query, keys, (((1,), (1,)), ((), ())), preferred_element_type=jnp.float32
         )
-        floor = floor_ref[qrows, :] - ((4 - d) * tokens + first)
+        floor = floor_ref[qrows, :] - ((REACH - d) * tokens + first)
         floor = jnp.concatenate([floor] * (size // 128), axis=1)
         column = lax.broadcasted_iota(jnp.int32, (QB, size), 1)
         allowed = column >= floor
@@ -288,50 +348,263 @@
         else:
             total[slot] += product
 
-    for d in range(5):
-        copies[d].wait()
+    for d in (0, 1, 4, 2, 3):
+        if d > 0:
+            moves[d].wait_recv()
 
         def pair(t, carry):
             g, qb = lax.div(t, blocks), lax.rem(t, blocks)
             if d == 0:
                 chunk(0, g, qb, qb * QB, QB, diagonal=True, fresh=True)
                 lax.fori_loop(0, qb, lambda k, c: (chunk(0, g, qb, k * QB, QB), c)[1], 0)
-            elif d < 4:
+            elif d < REACH:
                 chunk(d, g, qb, 0, tokens // 2)
                 chunk(d, g, qb, tokens // 2, tokens // 2)
             else:
                 lax.fori_loop(qb, blocks, lambda k, c: (chunk(4, g, qb, k * QB, QB), c)[1], 0)
+            if d == 3:
                 slot = g * blocks + qb
                 result = (total[slot, :, :HD] / total[slot, :, HD:]).astype(out_ref.dtype)
-                qrows = pl.ds(pl.multiple_of(qb * QB, QB), QB)
-                out_ref[qrows, lanes(g * 256, 128)] = result[:QB]
-                out_ref[qrows, lanes(g * 256 + 128, 128)] = result[QB:]
+                out_ref[block_rows(qb), lanes(g * 256, 128)] = result[:QB]
+                out_ref[block_rows(qb), lanes(g * 256 + 128, 128)] = result[QB:]
             return carry
 
         lax.fori_loop(0, 2 * blocks, pair, 0)
-
-
-def attention(query, floor, sources):
-    tokens = query.shape[0]
+    save.wait()
+    for d in range(1, REACH + 1):
+        moves[d].wait_send()
+
+
+def attention(tok_all, w_all, gain, cosine, sine, floor):
+    parts, tokens, width = tok_all.shape
+    columns = w_all.shape[1]
+    half = columns // 2
     vmem_spec = pl.BlockSpec(memory_space=pltpu.VMEM)
     any_spec = pl.BlockSpec(memory_space=pl.ANY)
+    dma = pltpu.SemaphoreType.DMA
     return pl.pallas_call(
         attention_kernel,
-        out_shape=jax.ShapeDtypeStruct(query.shape, jnp.bfloat16),
-        in_specs=[vmem_spec, vmem_spec] + [any_spec] * 5,
-        out_specs=vmem_spec,
+        out_shape=(
+            jax.ShapeDtypeStruct((tokens, half), jnp.bfloat16),
+            jax.ShapeDtypeStruct((tokens, half), jnp.bfloat16),
+        ),
+        in_specs=[any_spec] * 2 + [vmem_spec] * 4,
+        out_specs=(vmem_spec, any_spec),
         scratch_shapes=[
-            pltpu.VMEM((5,) + sources[0].shape, jnp.bfloat16),
+            pltpu.VMEM(tok_all.shape, jnp.bfloat16),
+            pltpu.VMEM(w_all.shape, jnp.bfloat16),
+            pltpu.VMEM((tokens, half), jnp.bfloat16),
+            pltpu.VMEM((REACH + 1, tokens, half), jnp.bfloat16),
             pltpu.VMEM((8, 2 * QB, 256), jnp.float32),
-            pltpu.SemaphoreType.DMA((5,)),
+            dma((tokens // QB,)), dma((2,)), dma, dma((REACH + 1,)), dma((REACH + 1,)),
         ],
         cost_estimate=pl.CostEstimate(
-            flops=4 * tokens * 4352 * 128 * 8, bytes_accessed=8 << 20,
+            flops=4 * tokens * 4352 * 128 * 8, bytes_accessed=32 << 20,
             transcendentals=8 * tokens * 4352,
         ),
-        compiler_params=pltpu.CompilerParams(vmem_limit_bytes=40 << 20),
+        compiler_params=pltpu.CompilerParams(
+            vmem_limit_bytes=56 << 20, has_side_effects=True
+        ),
         name="attention",
-    )(query, floor, *sources)
+    )(tok_all, w_all, gain, cosine, sine, floor)
+
+
+def tail_kernel(
+    attn_ref, w_ref, tok_ref, gain_ref, pages_hbm,
+    mixed_ref, pages_in,
+    give, take, stage, far, near, kept, squares,
+    p_send, p_recv, own_sem, c_send, c_recv, f_send, f_recv, n_send, n_recv, s_send, s_recv,
+):
+    wide = lax.axis_index("wide")
+    narrow = lax.axis_index("narrow")
+    z, core = lax.div(narrow, 2), lax.rem(narrow, 2)
+    count = NX * NY
+    tokens = attn_ref.shape[0]
+    mid = tokens // 2
+    low, high = pl.ds(0, mid), pl.ds(mid, mid)
+    sibling = {"narrow": z * 2 + (1 - core)}
+
+    def at_z(step):
+        return lax.rem(z + step + NZ, NZ)
+
+    def remote(src, dst, send, recv, where):
+        copy = pltpu.make_async_remote_copy(
+            src_ref=src, dst_ref=dst, send_sem=send, recv_sem=recv,
+            device_id=where, device_id_type=MESH,
+        )
+        copy.start()
+        return copy
+
+    pages = [
+        remote(
+            pages_hbm.at[lax.rem(wide + other, count)], pages_in.at[wide],
+            p_send.at[other], p_recv.at[other], {"wide": lax.rem(wide + other, count)},
+        )
+        for other in range(1, count)
+    ]
+    own = pltpu.make_async_copy(pages_hbm.at[wide], pages_in.at[wide], own_sem)
+    own.start()
+
+    def term(index, rows):
+        weights = jnp.concatenate([w_ref[2 * index], w_ref[2 * index + 1]], axis=1)
+        return jnp.dot(
+            attn_ref[rows, :], weights, preferred_element_type=jnp.float32
+        ).astype(jnp.bfloat16)
+
+    def over_rows(body, first=0, size=tokens):
+        def step(b, carry):
+            body(pl.ds(pl.multiple_of(first + b * QB, QB), QB))
+            return carry
+
+        lax.fori_loop(0, size // QB, step, 0)
+
+    steps = (2, 1, -1, 0)
+    passes = []
+    for i, step in enumerate(steps):
+        index = at_z(step) * 2 + (1 - core)
+
+        def fill(rows, i=i, index=index):
+            give[i, rows, :] = term(index, rows)
+
+        over_rows(fill)
+        passes.append(remote(give.at[i], take.at[i], c_send.at[i], c_recv.at[i], sibling))
+
+    def own_sum(i, rows):
+        mine = term(at_z(steps[i]) * 2 + core, rows)
+        return mine.astype(jnp.float32) + take[i, rows, :].astype(jnp.float32)
+
+    def put(i):
+        def body(rows):
+            stage[i, rows, :] = own_sum(i, rows).astype(jnp.bfloat16)
+
+        return body
+
+    ahead, behind = {"narrow": at_z(1) * 2 + core}, {"narrow": at_z(-1) * 2 + core}
+    passes[0].wait_recv()
+    over_rows(put(0), 0, mid)
+    far_up = remote(stage.at[0, low], far.at[0], f_send.at[0], f_recv.at[0], ahead)
+    over_rows(put(0), mid, mid)
+    far_down = remote(stage.at[0, high], far.at[1], f_send.at[1], f_recv.at[1], behind)
+    passes[1].wait_recv()
+    over_rows(put(1), mid, mid)
+    near_a = remote(stage.at[1, high], near.at[0, high], n_send.at[0], n_recv.at[0], ahead)
+    passes[2].wait_recv()
+    over_rows(put(2), 0, mid)
+    near_b = remote(stage.at[2, low], near.at[1, low], n_send.at[1], n_recv.at[1], behind)
+
+    far_up.wait_recv()
+
+    def with_far_up(rows):
+        stage[1, rows, :] = (own_sum(1, rows) + far[0, rows, :].astype(jnp.float32)).astype(
+            jnp.bfloat16
+        )
+
+    over_rows(with_far_up, 0, mid)
+    near_c = remote(stage.at[1, low], near.at[0, low], n_send.at[2], n_recv.at[2], ahead)
+    far_down.wait_recv()
+
+    def with_far_down(b, carry):
+        rows = pl.ds(pl.multiple_of(mid + b * QB, QB), QB)
+        source = pl.ds(pl.multiple_of(b * QB, QB), QB)
+        stage[2, rows, :] = (own_sum(2, rows) + far[1, source, :].astype(jnp.float32)).astype(
+            jnp.bfloat16
+        )
+        return carry
+
+    lax.fori_loop(0, mid // QB, with_far_down, 0)
+    near_d = remote(stage.at[2, high], near.at[1, high], n_send.at[3], n_recv.at[3], behind)
+    passes[3].wait_recv()
+
+    def keep(rows):
+        kept[rows, :] = own_sum(3, rows)
+
+    over_rows(keep)
+    for copy in (near_a, near_b, near_c, near_d):
+        copy.wait_recv()
+
+    ones = jnp.ones((8, tok_ref.shape[1]), jnp.float32)
+
+    def finish(rows):
+        value = (
+            kept[rows, :]
+            + near[0, rows, :].astype(jnp.float32)
+            + near[1, rows, :].astype(jnp.float32)
+        )
+        kept[rows, :] = value
+        squares[0, :, rows] = lax.dot_general(
+            ones, value * value, (((1,), (1,)), ((), ())),
+            precision=lax.Precision.HIGHEST, preferred_element_type=jnp.float32,
+        )
+
+    over_rows(finish)
+    sums = [
+        remote(
+            squares.at[0], squares.at[other], s_send.at[other], s_recv.at[other],
+            {"narrow": lax.rem(narrow + other, NZ * 2)},
+        )
+        for other in range(1, NZ * 2)
+    ]
+    for copy in sums:
+        copy.wait_recv()
+    pick = jnp.full((8, 128), 0.125, jnp.float32)
+
+    def emit(rows):
+        whole = squares[0, :, rows]
+        for other in range(1, NZ * 2):
+            whole += squares[other, :, rows]
+        column = lax.dot_general(
+            whole, pick, (((0,), (0,)), ((), ())),
+            precision=lax.Precision.HIGHEST, preferred_element_type=jnp.float32,
+        )
+        scale = lax.rsqrt(column / D + NORM_EPSILON)[:, 0:1]
+        mixed_ref[rows, :] = (
+            tok_ref[rows, :].astype(jnp.float32)
+            + kept[rows, :] * scale * gain_ref[0:1, :].astype(jnp.float32)
+        ).astype(jnp.bfloat16)
+
+    over_rows(emit)
+    for copy in pages:
+        copy.wait_recv()
+    own.wait()
+    for copy in pages + passes + sums:
+        copy.wait_send()
+    for copy in (far_up, far_down, near_a, near_b, near_c, near_d):
+        copy.wait_send()
+
+
+def tail(attn, w_out_all, tokens, post_gain, outgoing):
+    rows, width = tokens.shape
+    vmem_spec = pl.BlockSpec(memory_space=pltpu.VMEM)
+    any_spec = pl.BlockSpec(memory_space=pl.ANY)
+    dma = pltpu.SemaphoreType.DMA
+    bf16 = jnp.bfloat16
+    return pl.pallas_call(
+        tail_kernel,
+        out_shape=(
+            jax.ShapeDtypeStruct(tokens.shape, bf16),
+            jax.ShapeDtypeStruct(outgoing.shape, bf16),
+        ),
+        in_specs=[vmem_spec] * 4 + [any_spec],
+        out_specs=(vmem_spec, any_spec),
+        scratch_shapes=[
+            pltpu.VMEM((4, rows, width), bf16),
+            pltpu.VMEM((4, rows, width), bf16),
+            pltpu.VMEM((3, rows, width), bf16),
+            pltpu.VMEM((2, rows // 2, width), bf16),
+            pltpu.VMEM((2, rows, width), bf16),
+            pltpu.VMEM((rows, width), jnp.float32),
+            pltpu.VMEM((8, 8, rows), jnp.float32),
+            dma((16,)), dma((16,)), dma, dma((4,)), dma((4,)), dma((2,)), dma((2,)),
+            dma((4,)), dma((4,)), dma((8,)), dma((8,)),
+        ],
+        cost_estimate=pl.CostEstimate(
+            flops=2 * rows * 512 * D, bytes_accessed=24 << 20, transcendentals=0
+        ),
+        compiler_params=pltpu.CompilerParams(
+            vmem_limit_bytes=56 << 20, has_side_effects=True
+        ),
+        name="tail",
+    )(attn, w_out_all, tokens, post_gain, outgoing)
 
 
 def local(tokens, segment_ids, page_table, pre_gain, post_gain, w_query, w_key, w_value, w_out):
@@ -339,18 +612,18 @@
     shard_count = lax.axis_size("wide")
     shard_index = lax.axis_index("wide")
     block_count = page_table.shape[0]
+    pairs_here = w_key.shape[1] // HD
     seg_rows = segment_ids.reshape(8, tok_w // 8)
     table_row = jnp.pad(page_table[None, :], ((0, 7), (0, tok_w // 8 - block_count)))
     meta = jnp.concatenate([seg_rows, table_row], axis=0)
-    gain_in = jnp.pad(pre_gain[None, :], ((0, 15), (0, 64)))
-    weights = jnp.concatenate([w_query, w_key, w_value], axis=1)
+    gain_in = jnp.pad(pre_gain[None, :], ((0, 15), (0, 0)))
+    columns = []
+    for g in range(pairs_here):
+        columns += [w_key[:, g * HD : (g + 1) * HD], w_value[:, g * HD : (g + 1) * HD]]
+    weights = jnp.concatenate(columns + [w_query], axis=1)
     tok_all, w_all, meta_all, gain_all = gather_all(tokens, weights, meta, gain_in)
-
-    residual = tokens.astype(jnp.float32)
-    gathered = jnp.transpose(tok_all, (1, 0, 2)).reshape(tok_w, D)
-    features = gathered.astype(jnp.float32)
-    gain = gain_all[:, 0, : pre_gain.shape[0]].reshape(D)
-    normed = (features * rms_scale(features) * gain.astype(jnp.float32)).astype(jnp.bfloat16)
+    w_out_late, _ = lax.optimization_barrier((w_out, meta_all))
+    w_out_all = lax.all_gather(w_out_late, "wide", axis=0, tiled=False)
 
     labels = jnp.arange(SEGS, dtype=jnp.int32)
     all_ids = meta_all[:, :8, :].reshape(-1)
@@ -366,51 +639,25 @@
         -math.log(10000.0) * 2.0 * jnp.arange(half_width, dtype=jnp.float32) / HD
     )
     angle_table = positions.astype(jnp.float32)[:, None] * inverse_freq[None, :]
-    cosine = jnp.cos(angle_table)[:, None, :]
-    sine = jnp.sin(angle_table)[:, None, :]
-
-    heads_here = w_query.shape[1] // HD
-    pairs_here = w_key.shape[1] // HD
-    raw = jnp.dot(normed, w_all, preferred_element_type=jnp.float32)
-    q_width, k_width = w_query.shape[1], w_key.shape[1]
-    query_raw = raw[:, :q_width]
-    key_raw = raw[:, q_width : q_width + k_width]
-    value_raw = raw[:, q_width + k_width :]
-    keys_new = rotate_half(key_raw.reshape(tok_w, pairs_here, HD), cosine, sine).astype(
-        jnp.bfloat16
-    )
-    values_new = value_raw.reshape(tok_w, pairs_here, HD).astype(jnp.bfloat16)
-    paired = jnp.concatenate([keys_new, values_new], axis=2)
-    flat = paired.reshape(tok_w, pairs_here * 2 * HD)
-    reach_depth = min((WINDOW - 1) // tok_w + 1, shard_count - 1)
-    sources = [flat] + [shifted(flat, "wide", distance + 1) for distance in range(reach_depth)]
-    query_new = rotate_half(query_raw.reshape(tok_w, heads_here, HD), cosine, sine).astype(
-        jnp.bfloat16
-    ).reshape(tok_w, heads_here * HD)
+    cosine = jnp.cos(angle_table)
+    sine = jnp.sin(angle_table)
+    cosine = jnp.concatenate([cosine, cosine], axis=1)
+    sine = jnp.concatenate([-sine, sine], axis=1)
     key_floor = jnp.maximum(seg_start, token_index - WINDOW + 1) - (first_token - WINDOW)
     floor = jnp.broadcast_to(key_floor[:, None], (tok_w, 128))
-    w_out_late, _ = lax.optimization_barrier((w_out, w_all[:8, :128]))
-    w_out_all = lax.all_gather(w_out_late, "wide", axis=1, tiled=True)
-    attn_out = attention(query_new, floor, sources)
-
-    head_terms = jnp.dot(attn_out, w_out_all, preferred_element_type=jnp.float32)
-    projected = lax.psum_scatter(
-        head_terms.astype(jnp.bfloat16), "narrow", scatter_dimension=1, tiled=True
-    ).astype(jnp.float32)
-    square_sums = lax.psum(jnp.sum(projected * projected, axis=1), "narrow")
-    post_scale = lax.rsqrt(square_sums / D + NORM_EPSILON)
-    mixed = (residual + projected * post_scale[:, None] * post_gain.astype(jnp.float32)).astype(
-        jnp.bfloat16
-    )
+    attn_out, flat = attention(tok_all, w_all, gain_all, cosine, sine, floor)
+
     page_len = tok_w // block_count
-    token_blocks = paired.reshape(block_count, page_len, pairs_here, 2 * HD)
+    token_blocks = flat.reshape(block_count, page_len, pairs_here, 2 * HD)
     owners = page_table // block_count
     shard_ids = jnp.arange(shard_count, dtype=jnp.int32)
     send_pick = (owners[None, :] == shard_ids[:, None]).astype(jnp.bfloat16)
     outgoing = jnp.einsum(
         "sj,jpgc->sgpc", send_pick, token_blocks, preferred_element_type=jnp.float32
     ).astype(jnp.bfloat16)
-    incoming = lax.all_to_all(outgoing, "wide", split_axis=0, concat_axis=0, tiled=True)
+    mixed, incoming = tail(
+        attn_out, w_out_all, tokens, jnp.pad(post_gain[None, :], ((0, 15), (0, 0))), outgoing
+    )
     my_pages = shard_index * block_count + jnp.arange(block_count, dtype=jnp.int32)
     found_page = table_all[None, :] == my_pages[:, None]
     anchor = jnp.sum(

time: 397 us -> 355 us (0.89)
  Pallas kernels: 126 us -> 310 us
  waiting for transfers between devices: 68.5 us -> 0.03 us
  starting transfers between devices: 59.2 us -> 0.04 us
  other arithmetic: 41.9 us -> 4.36 us
  local copies, waits for them, and re-layouts: 48.4 us -> 21.3 us
  matrix products: 24.2 us -> 3.88 us
  blocking collectives: 13.2 us -> 0 us
    pallas_call x1 -> x2, Pallas kernels: 37.7 us -> 241 us  [the longest x1 134 us: tail(): pl.pallas_call(tail_kernel, out_shape=(jax.ShapeDtypeStruct(tokens.shape,...]
    all_to_all x1 -> x0, starting transfers between devices: 45.2 us -> none  [local(): lax.all_to_all(outgoing, 'wide', split_axis=0, concat_axis=0, tiled=True)]
    all_to_all x1 -> x0, waiting for transfers between devices: 25.2 us -> none  [local(): lax.all_to_all(outgoing, 'wide', split_axis=0, concat_axis=0, tiled=True)]
    convert_element_type x5 -> x0, local copies, waits for them, and re-layouts: 25.1 us -> none  [the longest x1 22.1 us: local(): features = gathered.astype(jnp.float32)]
    convert_element_type x5 -> x0, other arithmetic: 24.1 us -> none  [the longest x1 12.3 us: local(): features = gathered.astype(jnp.float32)]
    ppermute x4 -> x0, waiting for transfers between devices: 23.3 us -> none  [shifted(): lax.ppermute(value, axis, [(source, source + steps) for source in range(l...]
    dot_general x2 -> x0, matrix products: 22.2 us -> none  [the longest x1 12.7 us: local(): raw = jnp.dot(normed, w_all, preferred_element_type=jnp.float32)]
    reduce_scatter x1 -> x0, waiting for transfers between devices: 19.2 us -> none  [local(): lax.psum_scatter(head_terms.astype(jnp.bfloat16), 'narrow', scatter_dimen...]
  transfers between devices with their start and end apart: 7 -> 1, of which waited for: 4 -> 0; matrix products, arithmetic and copies ran while one was open for 24% -> 3% of each run, Pallas kernels for 32% -> 30%
where the time goes in v1:
time: 355 us; the launch traced here: 354 us
  Pallas kernels  310 us (87%)
  local copies, waits for them, and re-layouts  21.3 us (6%)
  between operations  14.3 us (4%)
  other arithmetic  4.36 us (1%)
  matrix products  3.88 us (1%)
    pallas_call x1, Pallas kernels, tail(): pl.pallas_call(tail_kernel, out_shape=(jax.ShapeDtypeStruct(tokens.shape,...  134 us
    pallas_call x1, Pallas kernels, attention(): pl.pallas_call(attention_kernel, out_shape=(jax.ShapeDtypeStruct((tokens,...  106 us
    pallas_call x1, Pallas kernels, gather_all(): pl.pallas_call(gather_kernel, out_shape=(jax.ShapeDtypeStruct((8, rows, w...  69.9 us
    all_gather x1, local copies, waits for them, and re-layouts, local(): w_out_all = lax.all_gather(w_out_late, 'wide', axis=0, tiled=False)  7.94 us
  transfers between devices with their start and end apart: 1, of which 0 were waited for; matrix products, arithmetic and copies ran while one was open for 3% of the time, Pallas kernels for 30%

profile of v1, /device:TPU:1, one launch (start us, length us, event | category | flops | bytes accessed | tf_op | source)
XLA Modules:
  0.0 354.3 jit_solution(9271845797784215770)
XLA Ops:
  7.2 0.0 all-gather.3.cloned.1.call-start
  7.3 2.6 copy.27.tok_ref
  10.1 0.7 pad.12.gain_ref
  10.7 0.6 pad_add_fusion.meta_ref
  11.3 69.9 %gather_all.1 = (bf16[8,1024,576]{2,1,0:T(8,128)(2,1)}, bf16[4608,1024]{1,0:T(8,128)(2,1)}, s32[16,16,128]{2,1,0:T(8,128)}, bf16[8,16,576]{2,1,0:T(8,128)(2,1)}) custom-call(bf16[1024,576]{1,0:T(8,128)(2,1)} %copy.27.tok_ref, bf16[288,1024]{1,0:T(8,128)(2,1)} %copy-done.1, s32[16,128]{1,0:T(8,128)} %pad_add_fusion.meta_ref, bf16[16,576]{1,0:T(8,128)(2,1)} %pad.12.gain_ref), custom_call_target="tpu_custom_call" | custom-call | tf_op jit(solution)/shard_map/gather_all/pallas_call | solution.py:203
  81.3 0.8 slice_bitcast_fusion
  82.1 0.2 convert_reduce_fusion
  82.3 0.1 select_reduce_fusion
  82.5 1.9 fusion.8
  84.4 1.3 pad_maximum_fusion
  85.7 1.0 broadcast_in_dim.55.floor_ref
  86.7 106.4 %attention.1 = (bf16[1024,512]{1,0:T(8,128)(2,1)}, bf16[1024,512]{1,0:T(8,128)(2,1)}) custom-call(bf16[8,1024,576]{2,1,0:T(8,128)(2,1)} %get-tuple-element.11.tok_hbm, bf16[4608,1024]{1,0:T(8,128)(2,1)} %get-tuple-element.12.w_hbm, bf16[8,16,576]{2,1,0:T(8,128)(2,1)} %get-tuple-element.13.gain_ref, f32[1024,128]{1,0:T(8,128)} %get-tuple-element.31.cos_ref, ...), custom_call_target="tpu_custom_call" | custom-call | flops 18253611008 | bytes 33554432 | tf_op jit(solution)/shard_map/attention/pallas_call | solution.py:385
  193.1 1.3 reshape.78
  194.5 0.9 fusion.6
  195.4 2.5 copy.46
  198.0 0.6 pad.13.gain_ref
  198.6 0.9 slice_reduce_fusion
  199.4 0.1 eq.60
  199.6 0.2 select_reduce_fusion.1
  199.8 7.9 %copy.28 = bf16[8192,288]{1,0:T(8,128)(2,1)} copy(bf16[8192,288]{0,1:T(8,128)(2,1)} %all-gather.3.cloned.1.call-done) | data formatting | bytes 9437184 | tf_op jit(solution)/shard_map/all_gather | solution.py:626
  207.7 134.2 %tail.1 = (bf16[1024,576]{1,0:T(8,128)(2,1)}, bf16[16,2,128,256]{3,2,1,0:T(8,128)(2,1)}) custom-call(bf16[1024,512]{1,0:T(8,128)(2,1)} %get-tuple-element.15.attn_ref, bf16[16,512,288]{2,1,0:T(8,128)(2,1)} %bitcast.18, bf16[1024,576]{1,0:T(8,128)(2,1)} %copy.27.tok_ref, bf16[16,576]{1,0:T(8,128)(2,1)} %pad.13.gain_ref, bf16[16,2,128,256]{3,2,1,0:T(8,128)(2,1)} %bitcast.19), custom_call_target="tpu_custom_call" | custom-call | flops 4831838208 | bytes 25165824 | tf_op jit(solution)/shard_map/tail/pallas_call | solution.py:581
  341.9 2.9 fusion.3
  344.9 1.2 copy.34
  346.1 1.4 copy.33
  (32 shorter events, 0.2 us)
Async XLA Ops:
  7.2 2.7 copy-start.3
  7.2 2.7 copy-start.4
  7.2 2.8 copy-start.6
  7.2 2.8 copy-start.2
  7.2 3.5 copy-start.5
  7.2 3.5 copy-start.8
  7.2 192.5 %all-gather.3.cloned.1.call-start = ((), (), s32[]{:S(2)}) async-start(), calls=%async_computation | async-start | bytes 5013504 | tf_op jit(solution)/shard_map/all_gather | solution.py:626
  10.0 1.3 copy-start.1
  195.4 2.6 copy-start.7
  341.9 4.2 %copy-start = (bf16[1024,576]{1,0:T(8,128)(2,1)S(1)}, bf16[1024,576]{1,0:T(8,128)(2,1)}, u32[]{:S(2)}) copy-start(bf16[1024,576]{1,0:T(8,128)(2,1)} %get-tuple-element.24) | copy-start | bytes 3538948
Sparse Core Ops, SparseCore 0:
  81.4 89.3 all-gather.2

commit v2 on v1

--- a/solution.py
+++ b/solution.py
@@ -290,13 +290,49 @@
     lax.fori_loop(0, blocks, key_block, 0)
     save = pltpu.make_async_copy(held.at[0], kv_hbm, kv_sem)
     save.start()
-    moves = {}
-    for d in (1, 4, 2, 3):
-        moves[d] = pltpu.make_async_remote_copy(
-            src_ref=held.at[0], dst_ref=held.at[d], send_sem=send.at[d], recv_sem=recv.at[d],
-            device_id={"wide": lax.rem(wide + d, count)}, device_id_type=MESH,
-        )
-        moves[d].start()
+    x, y = lax.div(wide, NY), lax.rem(wide, NY)
+    next_x = lax.rem(x + 1, NX) * NY + y
+    next_y = x * NY + lax.rem(y + 1, NY)
+    last_y = x * NY + lax.rem(y + NY - 1, NY)
+    inner = (y == 1) | (y == 2)
+
+    def move(kind, source, slot, where, c):
+        rows = block_rows(c)
+        return pltpu.make_async_remote_copy(
+            src_ref=held.at[source, rows], dst_ref=held.at[slot, rows],
+            send_sem=send.at[kind, c], recv_sem=recv.at[slot, c],
+            device_id={"wide": where}, device_id_type=MESH,
+        )
+
+    def along_x(c):
+        return move(0, 0, 4, next_x, c)
+
+    def up(source, c):
+        return move(1, source, 1, next_y, c)
+
+    def down(source, c):
+        return move(2, source, 3, last_y, c)
+
+    def pass_up(c):
+        return move(3, 1, 2, next_y, c)
+
+    def pass_down(c):
+        return move(4, 3, 2, last_y, c)
+
+    def begin(c, carry):
+        along_x(c).start()
+
+        @pl.when(y < NY - 1)
+        def _():
+            up(0, c).start()
+
+        @pl.when(y == 0)
+        def _():
+            down(0, c).start()
+
+        return carry
+
+    lax.fori_loop(0, blocks, begin, 0)
     loads_w[1].wait()
 
     def query_block(b, carry):
@@ -348,37 +384,91 @@
         else:
             total[slot] += product
 
-    for d in (0, 1, 4, 2, 3):
-        if d > 0:
-            moves[d].wait_recv()
-
+    def own_pair(t, carry):
+        g, qb = lax.div(t, blocks), lax.rem(t, blocks)
+        chunk(0, g, qb, qb * QB, QB, diagonal=True, fresh=True)
+        lax.fori_loop(0, qb, lambda k, c: (chunk(0, g, qb, k * QB, QB), c)[1], 0)
+        return carry
+
+    def segment(d, k, pairs):
         def pair(t, carry):
-            g, qb = lax.div(t, blocks), lax.rem(t, blocks)
-            if d == 0:
-                chunk(0, g, qb, qb * QB, QB, diagonal=True, fresh=True)
-                lax.fori_loop(0, qb, lambda k, c: (chunk(0, g, qb, k * QB, QB), c)[1], 0)
-            elif d < REACH:
-                chunk(d, g, qb, 0, tokens // 2)
-                chunk(d, g, qb, tokens // 2, tokens // 2)
-            else:
-                lax.fori_loop(qb, blocks, lambda k, c: (chunk(4, g, qb, k * QB, QB), c)[1], 0)
-            if d == 3:
-                slot = g * blocks + qb
-                result = (total[slot, :, :HD] / total[slot, :, HD:]).astype(out_ref.dtype)
-                out_ref[block_rows(qb), lanes(g * 256, 128)] = result[:QB]
-                out_ref[block_rows(qb), lanes(g * 256 + 128, 128)] = result[QB:]
+            chunk(d, lax.rem(t, 2), lax.div(t, 2), k * QB, QB)
             return carry
 
-        lax.fori_loop(0, 2 * blocks, pair, 0)
+        lax.fori_loop(0, pairs, pair, 0)
+
+    lax.fori_loop(0, 2 * blocks, own_pair, 0)
+
+    def step(i, carry):
+        @pl.when(i < blocks)
+        def _():
+            along_x(i).wait_recv()
+
+            @pl.when(y == NY - 1)
+            def _():
+                up(4, i).start()
+
+            @pl.when(y > 0)
+            def _():
+                down(4, i).start()
+
+            up(0, i).wait_recv()
+
+            @pl.when(inner)
+            def _():
+                pass_up(i).start()
+
+            segment(4, i, 2 * (i + 1))
+            segment(1, i, 2 * blocks)
+
+        @pl.when((i >= 1) & (i < blocks + 1))
+        def _():
+            down(0, i - 1).wait_recv()
+
+            @pl.when(inner)
+            def _():
+                pass_down(i - 1).start()
+
+            segment(3, i - 1, 2 * blocks)
+
+        @pl.when(i >= 2)
+        def _():
+            pass_up(i - 2).wait_recv()
+            segment(2, i - 2, 2 * blocks)
+
+        return carry
+
+    lax.fori_loop(0, blocks + 2, step, 0)
+
+    def finish(t, carry):
+        g, qb = lax.div(t, blocks), lax.rem(t, blocks)
+        slot = g * blocks + qb
+        result = (total[slot, :, :HD] / total[slot, :, HD:]).astype(out_ref.dtype)
+        out_ref[block_rows(qb), lanes(g * 256, 128)] = result[:QB]
+        out_ref[block_rows(qb), lanes(g * 256 + 128, 128)] = result[QB:]
+        return carry
+
+    lax.fori_loop(0, 2 * blocks, finish, 0)
     save.wait()
-    for d in range(1, REACH + 1):
-        moves[d].wait_send()
+
+    def drain(c, carry):
+        along_x(c).wait_send()
+        up(0, c).wait_send()
+        down(0, c).wait_send()
+
+        @pl.when(inner)
+        def _():
+            pass_up(c).wait_send()
+            pass_down(c).wait_send()
+
+        return carry
+
+    lax.fori_loop(0, blocks, drain, 0)
 
 
 def attention(tok_all, w_all, gain, cosine, sine, floor):
     parts, tokens, width = tok_all.shape
-    columns = w_all.shape[1]
-    half = columns // 2
+    half = w_all.shape[1] // 3
     vmem_spec = pl.BlockSpec(memory_space=pltpu.VMEM)
     any_spec = pl.BlockSpec(memory_space=pl.ANY)
     dma = pltpu.SemaphoreType.DMA
@@ -392,11 +482,12 @@
         out_specs=(vmem_spec, any_spec),
         scratch_shapes=[
             pltpu.VMEM(tok_all.shape, jnp.bfloat16),
-            pltpu.VMEM(w_all.shape, jnp.bfloat16),
+            pltpu.VMEM((w_all.shape[0], 2 * half), jnp.bfloat16),
             pltpu.VMEM((tokens, half), jnp.bfloat16),
             pltpu.VMEM((REACH + 1, tokens, half), jnp.bfloat16),
             pltpu.VMEM((8, 2 * QB, 256), jnp.float32),
-            dma((tokens // QB,)), dma((2,)), dma, dma((REACH + 1,)), dma((REACH + 1,)),
+            dma((tokens // QB,)), dma((2,)), dma, dma((5, tokens // QB)),
+            dma((REACH + 1, tokens // QB)),
         ],
         cost_estimate=pl.CostEstimate(
             flops=4 * tokens * 4352 * 128 * 8, bytes_accessed=32 << 20,
@@ -410,9 +501,9 @@
 
 
 def tail_kernel(
-    attn_ref, w_ref, tok_ref, gain_ref, pages_hbm,
+    attn_ref, tok_ref, gain_ref, w_hbm, pages_hbm,
     mixed_ref, pages_in,
-    give, take, stage, far, near, kept, squares,
+    w, w_sem, give, take, stage, far, near, kept, squares,
     p_send, p_recv, own_sem, c_send, c_recv, f_send, f_recv, n_send, n_recv, s_send, s_recv,
 ):
     wide = lax.axis_index("wide")
@@ -445,10 +536,23 @@
     own = pltpu.make_async_copy(pages_hbm.at[wide], pages_in.at[wide], own_sem)
     own.start()
 
-    def term(index, rows):
-        weights = jnp.concatenate([w_ref[2 * index], w_ref[2 * index + 1]], axis=1)
-        return jnp.dot(
-            attn_ref[rows, :], weights, preferred_element_type=jnp.float32
+    steps = (2, 1, -1, 0)
+    depth, width = attn_ref.shape[1], tok_ref.shape[1]
+    loads = []
+    for slot in range(8):
+        index = at_z(steps[slot % 4]) * 2 + ((1 - core) if slot < 4 else core)
+        source = pl.ds(pl.multiple_of(index * width, width), width)
+        loads.append(
+            pltpu.make_async_copy(
+                w_hbm.at[source, pl.ds(w_hbm.shape[1] - depth, depth)], w.at[slot], w_sem.at[slot]
+            )
+        )
+        loads[-1].start()
+
+    def term(slot, rows):
+        return lax.dot_general(
+            attn_ref[rows, :], w[slot], (((1,), (1,)), ((), ())),
+            preferred_element_type=jnp.float32,
         ).astype(jnp.bfloat16)
 
     def over_rows(body, first=0, size=tokens):
@@ -458,19 +562,18 @@
 
         lax.fori_loop(0, size // QB, step, 0)
 
-    steps = (2, 1, -1, 0)
     passes = []
-    for i, step in enumerate(steps):
-        index = at_z(step) * 2 + (1 - core)
-
-        def fill(rows, i=i, index=index):
-            give[i, rows, :] = term(index, rows)
+    for i in range(4):
+        loads[i].wait()
+
+        def fill(rows, i=i):
+            give[i, rows, :] = term(i, rows)
 
         over_rows(fill)
         passes.append(remote(give.at[i], take.at[i], c_send.at[i], c_recv.at[i], sibling))
 
     def own_sum(i, rows):
-        mine = term(at_z(steps[i]) * 2 + core, rows)
+        mine = term(4 + i, rows)
         return mine.astype(jnp.float32) + take[i, rows, :].astype(jnp.float32)
 
     def put(i):
@@ -480,6 +583,8 @@
         return body
 
     ahead, behind = {"narrow": at_z(1) * 2 + core}, {"narrow": at_z(-1) * 2 + core}
+    for i in range(4, 8):
+        loads[i].wait()
     passes[0].wait_recv()
     over_rows(put(0), 0, mid)
     far_up = remote(stage.at[0, low], far.at[0], f_send.at[0], f_recv.at[0], ahead)
@@ -572,7 +677,7 @@
         copy.wait_send()
 
 
-def tail(attn, w_out_all, tokens, post_gain, outgoing):
+def tail(attn, w_all, tokens, post_gain, outgoing):
     rows, width = tokens.shape
     vmem_spec = pl.BlockSpec(memory_space=pltpu.VMEM)
     any_spec = pl.BlockSpec(memory_space=pl.ANY)
@@ -584,9 +689,11 @@
             jax.ShapeDtypeStruct(tokens.shape, bf16),
             jax.ShapeDtypeStruct(outgoing.shape, bf16),
         ),
-        in_specs=[vmem_spec] * 4 + [any_spec],
+        in_specs=[vmem_spec] * 3 + [any_spec] * 2,
         out_specs=(vmem_spec, any_spec),
         scratch_shapes=[
+            pltpu.VMEM((8, width, attn.shape[1]), bf16),
+            dma((8,)),
             pltpu.VMEM((4, rows, width), bf16),
             pltpu.VMEM((4, rows, width), bf16),
             pltpu.VMEM((3, rows, width), bf16),
@@ -604,7 +711,7 @@
             vmem_limit_bytes=56 << 20, has_side_effects=True
         ),
         name="tail",
-    )(attn, w_out_all, tokens, post_gain, outgoing)
+    )(attn, tokens, post_gain, w_all, outgoing)
 
 
 def local(tokens, segment_ids, page_table, pre_gain, post_gain, w_query, w_key, w_value, w_out):
@@ -620,11 +727,8 @@
     columns = []
     for g in range(pairs_here):
         columns += [w_key[:, g * HD : (g + 1) * HD], w_value[:, g * HD : (g + 1) * HD]]
-    weights = jnp.concatenate(columns + [w_query], axis=1)
+    weights = jnp.concatenate(columns + [w_query, jnp.transpose(w_out)], axis=1)
     tok_all, w_all, meta_all, gain_all = gather_all(tokens, weights, meta, gain_in)
-    w_out_late, _ = lax.optimization_barrier((w_out, meta_all))
-    w_out_all = lax.all_gather(w_out_late, "wide", axis=0, tiled=False)
-
     labels = jnp.arange(SEGS, dtype=jnp.int32)
     all_ids = meta_all[:, :8, :].reshape(-1)
     table_all = meta_all[:, 8, :block_count].reshape(-1)
@@ -656,7 +760,7 @@
         "sj,jpgc->sgpc", send_pick, token_blocks, preferred_element_type=jnp.float32
     ).astype(jnp.bfloat16)
     mixed, incoming = tail(
-        attn_out, w_out_all, tokens, jnp.pad(post_gain[None, :], ((0, 15), (0, 0))), outgoing
+        attn_out, w_all, tokens, jnp.pad(post_gain[None, :], ((0, 15), (0, 0))), outgoing
     )
     my_pages = shard_index * block_count + jnp.arange(block_count, dtype=jnp.int32)
     found_page = table_all[None, :] == my_pages[:, None]

time: 355 us -> 295 us (0.83)
  Pallas kernels: 310 us -> 265 us
  between operations: 14.3 us -> 0.79 us
    pallas_call x1, Pallas kernels: 134 us -> 75.3 us  [tail(): pl.pallas_call(tail_kernel, out_shape=(jax.ShapeDtypeStruct(tokens.shape,...]
    pallas_call x1, Pallas kernels: 69.9 us -> 90 us  [gather_all(): pl.pallas_call(gather_kernel, out_shape=(jax.ShapeDtypeStruct((8, rows, w...]
    all_gather x1 -> x0, local copies, waits for them, and re-layouts: 7.94 us -> none  [local(): w_out_all = lax.all_gather(w_out_late, 'wide', axis=0, tiled=False)]
    pallas_call x1, Pallas kernels: 106 us -> 100 us  [attention(): pl.pallas_call(attention_kernel, out_shape=(jax.ShapeDtypeStruct((tokens,...]
    unnamed x25 -> x16, local copies, waits for them, and re-layouts: 5.33 us -> 9.86 us
  transfers between devices with their start and end apart: 1 -> 0, of which waited for: 0 -> 0; matrix products, arithmetic and copies ran while one was open for 3% -> 0% of each run, Pallas kernels for 30% -> 0%
where the time goes in v2:
time: 295 us; the launch traced here: 294 us
  Pallas kernels  265 us (90%)
  local copies, waits for them, and re-layouts  20.1 us (7%)
  other arithmetic  5.79 us (2%)
    pallas_call x1, Pallas kernels, attention(): pl.pallas_call(attention_kernel, out_shape=(jax.ShapeDtypeStruct((tokens,...  100 us
    pallas_call x1, Pallas kernels, gather_all(): pl.pallas_call(gather_kernel, out_shape=(jax.ShapeDtypeStruct((8, rows, w...  90 us
    pallas_call x1, Pallas kernels, tail(): pl.pallas_call(tail_kernel, out_shape=(jax.ShapeDtypeStruct(tokens.shape,...  75.3 us
    unnamed x16, local copies, waits for them, and re-layouts  9.86 us

profile of v2, /device:TPU:1, one launch (start us, length us, event | category | flops | bytes accessed | tf_op | source)
XLA Modules:
  0.0 294.3 jit_solution(14974133875043114552)
XLA Ops:
  0.7 0.8 and_select_fusion.1
  1.4 0.7 broadcast_in_dim.33
  2.8 1.3 pad_add_fusion.meta_ref
  5.3 0.9 slice_dynamic-update-slice_fusion.3
  6.2 0.9 slice_dynamic-update-slice_fusion.2
  7.1 0.9 slice_dynamic-update-slice_fusion.1
  8.0 0.9 slice_dynamic-update-slice_fusion
  8.9 1.0 constant_dynamic-update-slice_fusion
  9.9 1.0 bitcast_dynamic-update-slice_fusion.w_ref
  11.0 1.5 copy.25.tok_ref
  12.5 90.0 %gather_all.1 = (bf16[8,1024,576]{2,1,0:T(8,128)(2,1)}, bf16[4608,1536]{1,0:T(8,128)(2,1)}, s32[16,16,128]{2,1,0:T(8,128)}, bf16[8,16,576]{2,1,0:T(8,128)(2,1)}) custom-call(bf16[1024,576]{1,0:T(8,128)(2,1)} %copy.25.tok_ref, bf16[288,1536]{1,0:T(8,128)(2,1)} %copy-done.2, s32[16,128]{1,0:T(8,128)} %pad_add_fusion.meta_ref, bf16[16,576]{1,0:T(8,128)(2,1)} %pad.12.gain_ref), custom_call_target="tpu_custom_call" | custom-call | tf_op jit(solution)/shard_map/gather_all/pallas_call | solution.py:203
  102.4 0.9 slice_reduce_fusion
  103.3 0.8 slice_bitcast_fusion
  104.8 1.0 broadcast_in_dim.55.floor_ref
  105.8 1.9 fusion.8
  107.7 1.3 pad_maximum_fusion
  109.0 100.2 %attention.1 = (bf16[1024,512]{1,0:T(8,128)(2,1)}, bf16[1024,512]{1,0:T(8,128)(2,1)}) custom-call(bf16[8,1024,576]{2,1,0:T(8,128)(2,1)} %get-tuple-element.10.tok_hbm, bf16[4608,1536]{1,0:T(8,128)(2,1)} %get-tuple-element.11.w_hbm, bf16[8,16,576]{2,1,0:T(8,128)(2,1)} %get-tuple-element.12.gain_ref, f32[1024,128]{1,0:T(8,128)} %get-tuple-element.29.cos_ref, ...), custom_call_target="tpu_custom_call" | custom-call | flops 18253611008 | bytes 33554432 | tf_op jit(solution)/shard_map/attention/pallas_call | solution.py:475
  209.2 1.3 reshape.78
  210.6 0.9 fusion.6
  211.5 2.5 copy.43
  214.1 75.3 %tail.1 = (bf16[1024,576]{1,0:T(8,128)(2,1)}, bf16[16,2,128,256]{3,2,1,0:T(8,128)(2,1)}) custom-call(bf16[1024,512]{1,0:T(8,128)(2,1)} %get-tuple-element.14.attn_ref, bf16[1024,576]{1,0:T(8,128)(2,1)} %copy.25.tok_ref, bf16[16,576]{1,0:T(8,128)(2,1)} %pad.13.gain_ref, bf16[4608,1536]{1,0:T(8,128)(2,1)} %get-tuple-element.11.w_hbm, ...), custom_call_target="tpu_custom_call" | custom-call | flops 4831838208 | bytes 25165824 | tf_op jit(solution)/shard_map/tail/pallas_call | solution.py:686
  289.4 2.5 copy.30
  291.9 1.2 fusion.3
  293.1 1.2 copy.31
  (19 shorter events, 2.5 us)
Async XLA Ops:
  0.6 10.3 %copy-start.1 = (bf16[1024,576]{0,1:T(8,128)(2,1)S(1)}, bf16[1024,576]{0,1:T(8,128)(2,1)}, u32[]{:S(2)}) copy-start(bf16[1024,576]{0,1:T(8,128)(2,1)} %param.9) | copy-start | bytes 3538948
  10.9 1.5 copy-start.2
  10.9 93.7 %copy-start.3 = (s32[1024]{0:T(1024)S(1)}, s32[1024]{0:T(1024)}, u32[]{:S(2)}) copy-start(s32[1024]{0:T(1024)} %param.10) | copy-start | bytes 12292
  289.4 2.5 copy-start

commit v3 on v2

--- a/solution.py
+++ b/solution.py
@@ -22,88 +22,127 @@
 POST = SOFT_CAP * math.log2(math.e)
 
 
-def gather_kernel(
-    tok_ref, w_ref, meta_ref, gain_ref,
-    tok_all, w_all, meta_all, gain_all,
+QB = 256
+REACH = 4
+WAVES = 3
+
+
+def lanes(start, size):
+    return pl.ds(pl.multiple_of(start, 128), size)
+
+
+def front_kernel(
+    tok_ref, w_ref, meta_ref, gain_ref, ids_ref, freq_ref,
+    out_ref, kv_hbm, w_out_hbm, meta_out,
+    tok, w, meta_all, gain_all, cos_ref, sin_ref, floor_ref, query_all, held, total,
     w_send, w_recv, z_send, z_recv, c_send, c_recv, m_send, m_recv, g_send, g_recv, own_sem,
+    out_sem, send, recv,
 ):
     wide = lax.axis_index("wide")
     narrow = lax.axis_index("narrow")
     x, y = lax.div(wide, NY), lax.rem(wide, NY)
     z, core = lax.div(narrow, 2), lax.rem(narrow, 2)
     shard = w_ref.shape[0]
-    half = shard // 2
-    cols = w_ref.shape[1] // 2
-    rows = tok_ref.shape[0]
+    part_rows = shard // 2
+    half = w_ref.shape[1] // WAVES
+    parts, tokens, width = tok.shape
+    blocks = tokens // QB
+
+    def block_rows(b):
+        return pl.ds(pl.multiple_of(b * QB, QB), QB)
 
     def ring(position, count, step):
         return lax.rem(position + step + count, count)
 
-    def at_wide(x_new, y_new):
-        return {"wide": x_new * NY + y_new}
-
-    def remote(src, dst, send, recv, where):
-        return pltpu.make_async_remote_copy(
-            src_ref=src, dst_ref=dst, send_sem=send, recv_sem=recv,
+    started = []
+
+    def remote(src, dst, send_sem, recv_sem, where):
+        copy = pltpu.make_async_remote_copy(
+            src_ref=src, dst_ref=dst, send_sem=send_sem, recv_sem=recv_sem,
             device_id=where, device_id_type=MESH,
         )
-
-    def peer(part, stage, step):
-        if (part == 0) == (stage == 0):
-            return at_wide(ring(x, NX, step), y)
-        return at_wide(x, ring(y, NY, step))
-
-    def block(part, along, across):
-        if part == 0:
-            return ring(x, NX, along) * NY + ring(y, NY, across)
-        return ring(x, NX, across) * NY + ring(y, NY, along)
-
-    def rows_of(part, along, across):
-        return pl.ds(block(part, along, across) * shard + part * half, half)
-
-    def send(part, group, kind, along, across, own=False):
-        stage = 0 if group == 0 else 1
-        where = peer(part, stage, 1 if kind % 2 == 0 else -1)
-        there = rows_of(part, along, across)
-        if kind < 2:
-            span = slice(None)
-        else:
-            span = pl.ds((kind - 2) * cols, cols)
-        if own:
-            src = w_ref.at[pl.ds(part * half, half), span]
-        else:
-            src = w_all.at[there, span]
-        return remote(
-            src, w_all.at[there, span],
-            w_send.at[part, group, kind], w_recv.at[part, group, kind], where,
-        )
-
-    started = []
-
-    def start(copy):
         copy.start()
         started.append(copy)
         return copy
 
+    def peer(part, stage, step):
+        if (part == 0) == (stage == 0):
+            return {"wide": ring(x, NX, step) * NY + y}
+        return {"wide": x * NY + ring(y, NY, step)}
+
+    def rows_of(part, along, across):
+        if part == 0:
+            block = ring(x, NX, along) * NY + ring(y, NY, across)
+        else:
+            block = ring(x, NX, across) * NY + ring(y, NY, along)
+        return pl.ds(pl.multiple_of(block * shard + part * part_rows, 16), part_rows)
+
     sent = {}
 
-    def go(part, group, kind, along, across, own=False):
-        sent[part, group, kind] = start(send(part, group, kind, along, across, own))
+    def go(wave, part, group, kind, along, across, own=False):
+        where = peer(part, 0 if group == 0 else 1, 1 if kind % 2 == 0 else -1)
+        there = rows_of(part, along, across)
+        if kind < 2:
+            span = pl.ds(wave * half, half)
+        else:
+            span = pl.ds(wave * half + (kind - 2) * (half // 2), half // 2)
+        src = w_ref.at[pl.ds(part * part_rows, part_rows), span] if own else w.at[there, span]
+        sent[wave, part, group, kind] = remote(
+            src, w.at[there, span],
+            w_send.at[wave, part, group, kind], w_recv.at[wave, part, group, kind], where,
+        )
+
+    def got(wave, part, group, kind):
+        sent[wave, part, group, kind].wait_recv()
+
+    def wave_own(wave):
+        for group in (0, 1):
+            for part in (0, 1):
+                go(wave, part, group, 0, 0, 0, True)
+                go(wave, part, group, 1, 0, 0, True)
+
+    def wave_first(wave):
+        for kind, along, group in ((0, -1, 2), (1, 1, 3)):
+            for part in (0, 1):
+                got(wave, part, 0, kind)
+                go(wave, part, 0, 2 + kind, along, 0)
+                go(wave, part, group, 0, along, 0)
+                go(wave, part, group, 1, along, 0)
+
+    def wave_pass(wave, group, along):
+        for part in (0, 1):
+            got(wave, part, group, 0)
+            go(wave, part, group, 2, along, -1)
+            got(wave, part, group, 1)
+            go(wave, part, group, 3, along, 1)
+
+    def wave_far(wave):
+        for part in (0, 1):
+            got(wave, part, 0, 2)
+            got(wave, part, 0, 3)
+            go(wave, part, 4, 0, 2, 0)
+            go(wave, part, 4, 1, 2, 0)
+
+    def wave_end(wave):
+        for group in range(1, 5):
+            for part in (0, 1):
+                got(wave, part, group, 2)
+                got(wave, part, group, 3)
 
     toks = {}
 
     def zgo(kind, index, src, span):
         where = {"narrow": ring(z, NZ, 1 if kind % 2 == 0 else -1) * 2 + core}
-        toks[kind] = start(remote(src, tok_all.at[index, span], z_send.at[kind], z_recv.at[kind], where))
+        toks[kind] = remote(src, tok.at[index, span], z_send.at[kind], z_recv.at[kind], where)
 
     pair = {}
 
     def cgo(kind, index, src, span):
         where = {"narrow": z * 2 + (1 - core)}
-        pair[kind] = start(remote(src, tok_all.at[index, span], c_send.at[kind], c_recv.at[kind], where))
-
-    every = pl.ds(0, rows)
-    low, high = pl.ds(0, rows // 2), pl.ds(rows // 2, rows // 2)
+        pair[kind] = remote(src, tok.at[index, span], c_send.at[kind], c_recv.at[kind], where)
+
+    every = pl.ds(0, tokens)
+    low, high = pl.ds(0, tokens // 2), pl.ds(tokens // 2, tokens // 2)
 
     def zblock(step):
         return ring(z, NZ, step) * 2 + core
@@ -111,160 +150,86 @@
     small = []
     for other in range(1, NX * NY):
         target = lax.rem(wide + other, NX * NY)
-        small.append(start(remote(
-            meta_ref, meta_all.at[wide], m_send.at[other], m_recv.at[other], {"wide": target})))
+        small.append(remote(
+            meta_ref, meta_all.at[wide], m_send.at[other], m_recv.at[other], {"wide": target}))
     for other in range(1, NZ * 2):
         target = lax.rem(narrow + other, NZ * 2)
-        small.append(start(remote(
-            gain_ref, gain_all.at[narrow], g_send.at[other], g_recv.at[other], {"narrow": target})))
-
-    for part in (0, 1):
-        go(part, 0, 0, 0, 0, True)
-        go(part, 0, 1, 0, 0, True)
+        small.append(remote(
+            gain_ref, gain_all.at[narrow], g_send.at[other], g_recv.at[other], {"narrow": target}))
+    wave_own(0)
     zgo(0, narrow, tok_ref, every)
     zgo(1, narrow, tok_ref, every)
     cgo(0, narrow, tok_ref, every)
-    for part in (0, 1):
-        go(part, 1, 0, 0, 0, True)
-        go(part, 1, 1, 0, 0, True)
     local = [
-        pltpu.make_async_copy(w_ref, w_all.at[pl.ds(wide * shard, shard)], own_sem.at[0]),
-        pltpu.make_async_copy(tok_ref, tok_all.at[narrow], own_sem.at[1]),
+        pltpu.make_async_copy(w_ref, w.at[pl.ds(wide * shard, shard)], own_sem.at[0]),
+        pltpu.make_async_copy(tok_ref, tok.at[narrow], own_sem.at[1]),
         pltpu.make_async_copy(meta_ref, meta_all.at[wide], own_sem.at[2]),
         pltpu.make_async_copy(gain_ref, gain_all.at[narrow], own_sem.at[3]),
     ]
     for copy in local:
         copy.start()
-
-    for part in (0, 1):
-        sent[part, 0, 0].wait_recv()
-        go(part, 0, 2, -1, 0)
-        go(part, 2, 0, -1, 0)
-        go(part, 2, 1, -1, 0)
-    for part in (0, 1):
-        sent[part, 0, 1].wait_recv()
-        go(part, 0, 3, 1, 0)
-        go(part, 3, 0, 1, 0)
-        go(part, 3, 1, 1, 0)
-
-    toks[0].wait_recv()
-    zgo(2, zblock(-1), tok_all.at[zblock(-1), low], low)
-    cgo(1, zblock(-1), tok_all.at[zblock(-1)], every)
-    toks[1].wait_recv()
-    zgo(3, zblock(1), tok_all.at[zblock(1), high], high)
-    cgo(2, zblock(1), tok_all.at[zblock(1)], every)
-
-    for part in (0, 1):
-        sent[part, 1, 0].wait_recv()
-        go(part, 1, 2, 0, -1)
-        sent[part, 1, 1].wait_recv()
-        go(part, 1, 3, 0, 1)
-    for part in (0, 1):
-        sent[part, 0, 2].wait_recv()
-        sent[part, 0, 3].wait_recv()
-        go(part, 4, 0, 2, 0)
-        go(part, 4, 1, 2, 0)
-    for group, along in ((2, -1), (3, 1)):
-        for part in (0, 1):
-            sent[part, group, 0].wait_recv()
-            go(part, group, 2, along, -1)
-            sent[part, group, 1].wait_recv()
-            go(part, group, 3, along, 1)
-    toks[2].wait_recv()
-    cgo(3, zblock(2), tok_all.at[zblock(2), low], low)
-    toks[3].wait_recv()
-    cgo(4, zblock(2), tok_all.at[zblock(2), high], high)
-    for part in (0, 1):
-        sent[part, 4, 0].wait_recv()
-        go(part, 4, 2, 2, -1)
-        sent[part, 4, 1].wait_recv()
-        go(part, 4, 3, 2, 1)
-
-    for part in (0, 1):
-        for group in range(1, 5):
-            sent[part, group, 2].wait_recv()
-            sent[part, group, 3].wait_recv()
-    for kind in range(5):
-        pair[kind].wait_recv()
+    wave_first(0)
+
     for copy in small:
         copy.wait_recv()
     for copy in local:
         copy.wait()
-    for copy in started:
-        copy.wait_send()
-
-
-def gather_all(tokens, weights, meta, gain):
-    rows, width = tokens.shape
-    shard, columns = weights.shape
-    any_spec = pl.BlockSpec(memory_space=pl.ANY)
-    vmem_spec = pl.BlockSpec(memory_space=pltpu.VMEM)
-    dma = pltpu.SemaphoreType.DMA
-    return pl.pallas_call(
-        gather_kernel,
-        out_shape=(
-            jax.ShapeDtypeStruct((8, rows, width), tokens.dtype),
-            jax.ShapeDtypeStruct((16 * shard, columns), weights.dtype),
-            jax.ShapeDtypeStruct((16,) + meta.shape, meta.dtype),
-            jax.ShapeDtypeStruct((8,) + gain.shape, gain.dtype),
-        ),
-        in_specs=[vmem_spec] * 4,
-        out_specs=(any_spec,) * 4,
-        scratch_shapes=[
-            dma((2, 5, 4)), dma((2, 5, 4)), dma((4,)), dma((4,)), dma((5,)), dma((5,)),
-            dma((16,)), dma((16,)), dma((8,)), dma((8,)), dma((4,)),
-        ],
-        compiler_params=pltpu.CompilerParams(has_side_effects=True),
-        name="gather_all",
-    )(tokens, weights, meta, gain)
-
-
-QB = 256
-REACH = 4
-
-
-def lanes(start, size):
-    return pl.ds(pl.multiple_of(start, 128), size)
-
-
-def attention_kernel(
-    tok_hbm, w_hbm, gain_ref, cos_ref, sin_ref, floor_ref,
-    out_ref, kv_hbm,
-    tok, w, query_all, held, total, tok_sem, w_sem, kv_sem, send, recv,
-):
-    parts, tokens, width = tok.shape
-    blocks = tokens // QB
-    half = w.shape[1] // 2
-    wide = lax.axis_index("wide")
-    count = NX * NY
-
-    def block_rows(b):
-        return pl.ds(pl.multiple_of(b * QB, QB), QB)
-
-    def load_tok(b):
-        return pltpu.make_async_copy(
-            tok_hbm.at[:, block_rows(b), :], tok.at[:, block_rows(b), :], tok_sem.at[b]
-        )
-
-    loads_w = [
-        pltpu.make_async_copy(
-            w_hbm.at[:, pl.ds(part * half, half)], w.at[:, pl.ds(part * half, half)], w_sem.at[part]
-        )
-        for part in range(2)
+    save_meta = pltpu.make_async_copy(meta_all, meta_out, out_sem.at[2])
+    save_meta.start()
+    first_token = wide * tokens
+    all_ids = meta_all[:, 0:8, :]
+    firsts = [
+        jnp.sum((all_ids < label).astype(jnp.float32)).astype(jnp.int32)
+        for label in range(1, SEGS)
     ]
-    load_tok(0).start()
-    loads_w[0].start()
-    for b in range(1, blocks):
-        load_tok(b).start()
-    loads_w[1].start()
+
+    def tables(b, carry):
+        rows = block_rows(b)
+        ids = ids_ref[rows, :]
+        start = jnp.zeros((QB, 128), jnp.int32)
+        for label in range(1, SEGS):
+            start = jnp.where(ids == label, firsts[label - 1], start)
+        index = first_token + b * QB + lax.broadcasted_iota(jnp.int32, (QB, 128), 0)
+        angle = (index - start).astype(jnp.float32) * freq_ref[0:1, :]
+        cos_ref[rows, :] = jnp.cos(angle)
+        sin_ref[rows, :] = jnp.sin(angle) * freq_ref[1:2, :]
+        floor_ref[rows, :] = jnp.maximum(start, index - WINDOW + 1) - (first_token - WINDOW)
+        return carry
+
+    wave_pass(0, 1, 0)
+    wave_far(0)
+    toks[0].wait_recv()
+    zgo(2, zblock(-1), tok.at[zblock(-1), low], low)
+    cgo(1, zblock(-1), tok.at[zblock(-1)], every)
+    toks[1].wait_recv()
+    zgo(3, zblock(1), tok.at[zblock(1), high], high)
+    cgo(2, zblock(1), tok.at[zblock(1)], every)
+    wave_own(1)
+    lax.fori_loop(0, blocks, tables, 0)
+    wave_pass(0, 2, -1)
+    wave_pass(0, 3, 1)
+    wave_pass(0, 4, 2)
+    wave_first(1)
+    toks[2].wait_recv()
+    cgo(3, zblock(2), tok.at[zblock(2), low], low)
+    toks[3].wait_recv()
+    cgo(4, zblock(2), tok.at[zblock(2), high], high)
+    wave_pass(1, 1, 0)
+    wave_far(1)
+    wave_end(0)
+    for kind in range(5):
+        pair[kind].wait_recv()
+    for kind in range(5):
+        pair[kind].wait_send()
+    for kind in range(4):
+        toks[kind].wait_send()
+    done = [id(copy) for copy in list(pair.values()) + list(toks.values())]
+    started[:] = [copy for copy in started if id(copy) not in done]
 
     def rotated(value, rows):
         return value * cos_ref[rows, :] + pltpu.roll(value, HD // 2, 1) * sin_ref[rows, :]
 
-    loads_w[0].wait()
-
     def key_block(b, carry):
-        load_tok(b).wait()
         rows = block_rows(b)
         squares = jnp.zeros((QB, 1), jnp.float32)
         for n in range(parts):
@@ -274,7 +239,7 @@
         product = jnp.zeros((QB, half), jnp.float32)
         for n in range(parts):
             piece = tok[n, rows, :].astype(jnp.float32)
-            normed = (piece * scale * gain_ref[n, 0:1, :].astype(jnp.float32)).astype(jnp.bfloat16)
+            normed = (piece * scale * gain_all[n, 0:1, :].astype(jnp.float32)).astype(jnp.bfloat16)
             tok[n, rows, :] = normed
             product += jnp.dot(
                 normed, w[pl.ds(n * width, width), 0:half], preferred_element_type=jnp.float32
@@ -286,54 +251,6 @@
                 :, g * 256 + HD : g * 256 + 256
             ].astype(jnp.bfloat16)
         return carry
-
-    lax.fori_loop(0, blocks, key_block, 0)
-    save = pltpu.make_async_copy(held.at[0], kv_hbm, kv_sem)
-    save.start()
-    x, y = lax.div(wide, NY), lax.rem(wide, NY)
-    next_x = lax.rem(x + 1, NX) * NY + y
-    next_y = x * NY + lax.rem(y + 1, NY)
-    last_y = x * NY + lax.rem(y + NY - 1, NY)
-    inner = (y == 1) | (y == 2)
-
-    def move(kind, source, slot, where, c):
-        rows = block_rows(c)
-        return pltpu.make_async_remote_copy(
-            src_ref=held.at[source, rows], dst_ref=held.at[slot, rows],
-            send_sem=send.at[kind, c], recv_sem=recv.at[slot, c],
-            device_id={"wide": where}, device_id_type=MESH,
-        )
-
-    def along_x(c):
-        return move(0, 0, 4, next_x, c)
-
-    def up(source, c):
-        return move(1, source, 1, next_y, c)
-
-    def down(source, c):
-        return move(2, source, 3, last_y, c)
-
-    def pass_up(c):
-        return move(3, 1, 2, next_y, c)
-
-    def pass_down(c):
-        return move(4, 3, 2, last_y, c)
-
-    def begin(c, carry):
-        along_x(c).start()
-
-        @pl.when(y < NY - 1)
-        def _():
-            up(0, c).start()
-
-        @pl.when(y == 0)
-        def _():
-            down(0, c).start()
-
-        return carry
-
-    lax.fori_loop(0, blocks, begin, 0)
-    loads_w[1].wait()
 
     def query_block(b, carry):
         rows = block_rows(b)
@@ -348,7 +265,46 @@
             query_all[rows, h * HD : (h + 1) * HD] = rotated(value, rows).astype(jnp.bfloat16)
         return carry
 
-    lax.fori_loop(0, blocks, query_block, 0)
+    next_x = lax.rem(x + 1, NX) * NY + y
+    next_y = x * NY + lax.rem(y + 1, NY)
+    last_y = x * NY + lax.rem(y + NY - 1, NY)
+    inner = (y == 1) | (y == 2)
+
+    def move(kind, source, slot, where, c):
+        rows = block_rows(c)
+        return pltpu.make_async_remote_copy(
+            src_ref=held.at[source, rows], dst_ref=held.at[slot, rows],
+            send_sem=send.at[kind, c], recv_sem=recv.at[slot, c],
+            device_id={"wide": where}, device_id_type=MESH,
+        )
+
+    def along_x(c):
+        return move(0, 0, 4, next_x, c)
+
+    def up(source, c):
+        return move(1, source, 1, next_y, c)
+
+    def down(source, c):
+        return move(2, source, 3, last_y, c)
+
+    def pass_up(c):
+        return move(3, 1, 2, next_y, c)
+
+    def pass_down(c):
+        return move(4, 3, 2, last_y, c)
+
+    def begin(c, carry):
+        along_x(c).start()
+
+        @pl.when(y < NY - 1)
+        def _():
+            up(0, c).start()
+
+        @pl.when(y == 0)
+        def _():
+            down(0, c).start()
+
+        return carry
 
     def chunk(d, g, qb, first, size, diagonal=False, fresh=False):
         qrows = block_rows(qb)
@@ -397,6 +353,24 @@
 
         lax.fori_loop(0, pairs, pair, 0)
 
+    wave_own(2)
+    lax.fori_loop(0, 2, key_block, 0)
+    wave_pass(1, 2, -1)
+    wave_pass(1, 3, 1)
+    wave_pass(1, 4, 2)
+    wave_first(2)
+    lax.fori_loop(2, blocks, key_block, 0)
+    wave_pass(2, 1, 0)
+    wave_far(2)
+    save = pltpu.make_async_copy(held.at[0], kv_hbm, out_sem.at[0])
+    save.start()
+    wave_end(1)
+    lax.fori_loop(0, 2, query_block, 0)
+    wave_pass(2, 2, -1)
+    wave_pass(2, 3, 1)
+    lax.fori_loop(2, blocks, query_block, 0)
+    wave_pass(2, 4, 2)
+    lax.fori_loop(0, blocks, begin, 0)
     lax.fori_loop(0, 2 * blocks, own_pair, 0)
 
     def step(i, carry):
@@ -449,7 +423,11 @@
         return carry
 
     lax.fori_loop(0, 2 * blocks, finish, 0)
+    wave_end(2)
+    save_w = pltpu.make_async_copy(w.at[:, pl.ds(2 * half, half)], w_out_hbm, out_sem.at[1])
+    save_w.start()
     save.wait()
+    save_meta.wait()
 
     def drain(c, carry):
         along_x(c).wait_send()
@@ -464,40 +442,54 @@
         return carry
 
     lax.fori_loop(0, blocks, drain, 0)
-
-
-def attention(tok_all, w_all, gain, cosine, sine, floor):
-    parts, tokens, width = tok_all.shape
-    half = w_all.shape[1] // 3
+    for copy in started:
+        copy.wait_send()
+    save_w.wait()
+
+
+def front(tokens, weights, meta, gain, ids, freq):
+    rows, width = tokens.shape
+    shard, columns = weights.shape
+    half = columns // WAVES
     vmem_spec = pl.BlockSpec(memory_space=pltpu.VMEM)
     any_spec = pl.BlockSpec(memory_space=pl.ANY)
     dma = pltpu.SemaphoreType.DMA
+    bf16 = jnp.bfloat16
+    blocks = rows // QB
     return pl.pallas_call(
-        attention_kernel,
+        front_kernel,
         out_shape=(
-            jax.ShapeDtypeStruct((tokens, half), jnp.bfloat16),
-            jax.ShapeDtypeStruct((tokens, half), jnp.bfloat16),
+            jax.ShapeDtypeStruct((rows, half), bf16),
+            jax.ShapeDtypeStruct((rows, half), bf16),
+            jax.ShapeDtypeStruct((16 * shard, half), bf16),
+            jax.ShapeDtypeStruct((16,) + meta.shape, meta.dtype),
         ),
-        in_specs=[any_spec] * 2 + [vmem_spec] * 4,
-        out_specs=(vmem_spec, any_spec),
+        in_specs=[vmem_spec] * 6,
+        out_specs=(vmem_spec, any_spec, any_spec, any_spec),
         scratch_shapes=[
-            pltpu.VMEM(tok_all.shape, jnp.bfloat16),
-            pltpu.VMEM((w_all.shape[0], 2 * half), jnp.bfloat16),
-            pltpu.VMEM((tokens, half), jnp.bfloat16),
-            pltpu.VMEM((REACH + 1, tokens, half), jnp.bfloat16),
+            pltpu.VMEM((8, rows, width), bf16),
+            pltpu.VMEM((16 * shard, columns), bf16),
+            pltpu.VMEM((16,) + meta.shape, jnp.int32),
+            pltpu.VMEM((8,) + gain.shape, bf16),
+            pltpu.VMEM((rows, 128), jnp.float32),
+            pltpu.VMEM((rows, 128), jnp.float32),
+            pltpu.VMEM((rows, 128), jnp.int32),
+            pltpu.VMEM((rows, half), bf16),
+            pltpu.VMEM((REACH + 1, rows, half), bf16),
             pltpu.VMEM((8, 2 * QB, 256), jnp.float32),
-            dma((tokens // QB,)), dma((2,)), dma, dma((5, tokens // QB)),
-            dma((REACH + 1, tokens // QB)),
+            dma((3, 2, 5, 4)), dma((3, 2, 5, 4)), dma((4,)), dma((4,)), dma((5,)), dma((5,)),
+            dma((16,)), dma((16,)), dma((8,)), dma((8,)), dma((4,)),
+            dma((3,)), dma((5, blocks)), dma((REACH + 1, blocks)),
         ],
         cost_estimate=pl.CostEstimate(
-            flops=4 * tokens * 4352 * 128 * 8, bytes_accessed=32 << 20,
-            transcendentals=8 * tokens * 4352,
+            flops=4 * rows * 4352 * 128 * 8, bytes_accessed=32 << 20,
+            transcendentals=8 * rows * 4352,
         ),
         compiler_params=pltpu.CompilerParams(
-            vmem_limit_bytes=56 << 20, has_side_effects=True
+            vmem_limit_bytes=60 << 20, has_side_effects=True
         ),
-        name="attention",
-    )(tok_all, w_all, gain, cosine, sine, floor)
+        name="front",
+    )(tokens, weights, meta, gain, ids, freq)
 
 
 def tail_kernel(
@@ -728,28 +720,16 @@
     for g in range(pairs_here):
         columns += [w_key[:, g * HD : (g + 1) * HD], w_value[:, g * HD : (g + 1) * HD]]
     weights = jnp.concatenate(columns + [w_query, jnp.transpose(w_out)], axis=1)
-    tok_all, w_all, meta_all, gain_all = gather_all(tokens, weights, meta, gain_in)
-    labels = jnp.arange(SEGS, dtype=jnp.int32)
-    all_ids = meta_all[:, :8, :].reshape(-1)
-    table_all = meta_all[:, 8, :block_count].reshape(-1)
-    seg_firsts = jnp.sum((all_ids[:, None] < labels[None, :]).astype(jnp.int32), axis=0)
-    member = segment_ids[:, None] == labels[None, :]
-    seg_start = jnp.sum(jnp.where(member, seg_firsts[None, :], 0), axis=1)
-    first_token = shard_index * tok_w
-    token_index = first_token + jnp.arange(tok_w, dtype=jnp.int32)
-    positions = token_index - seg_start
     half_width = HD // 2
     inverse_freq = jnp.exp(
         -math.log(10000.0) * 2.0 * jnp.arange(half_width, dtype=jnp.float32) / HD
     )
-    angle_table = positions.astype(jnp.float32)[:, None] * inverse_freq[None, :]
-    cosine = jnp.cos(angle_table)
-    sine = jnp.sin(angle_table)
-    cosine = jnp.concatenate([cosine, cosine], axis=1)
-    sine = jnp.concatenate([-sine, sine], axis=1)
-    key_floor = jnp.maximum(seg_start, token_index - WINDOW + 1) - (first_token - WINDOW)
-    floor = jnp.broadcast_to(key_floor[:, None], (tok_w, 128))
-    attn_out, flat = attention(tok_all, w_all, gain_all, cosine, sine, floor)
+    signs = jnp.where(jnp.arange(HD) < half_width, -1.0, 1.0)
+    freq = jnp.zeros((8, HD), jnp.float32)
+    freq = freq.at[0].set(jnp.concatenate([inverse_freq, inverse_freq])).at[1].set(signs)
+    ids = jnp.broadcast_to(segment_ids[:, None], (tok_w, 128))
+    attn_out, flat, w_all, meta_all = front(tokens, weights, meta, gain_in, ids, freq)
+    table_all = meta_all[:, 8, :block_count].reshape(-1)
 
     page_len = tok_w // block_count
     token_blocks = flat.reshape(block_count, page_len, pairs_here, 2 * HD)

time: 295 us -> 272 us (0.922)
  Pallas kernels: 265 us -> 246 us
  other arithmetic: 5.79 us -> 2.34 us
    pallas_call x2 -> x1, Pallas kernels: 190 us -> 172 us  [front(): pl.pallas_call(front_kernel, out_shape=(jax.ShapeDtypeStruct((rows, half)...]
where the time goes in v3:
time: 272 us
  Pallas kernels  246 us (90%)
  local copies, waits for them, and re-layouts  20.1 us (7%)
    pallas_call x1, Pallas kernels, front(): pl.pallas_call(front_kernel, out_shape=(jax.ShapeDtypeStruct((rows, half)...  172 us
    pallas_call x1, Pallas kernels, tail(): pl.pallas_call(tail_kernel, out_shape=(jax.ShapeDtypeStruct(tokens.shape,...  74.5 us
    unnamed x16, local copies, waits for them, and re-layouts  9.8 us

profile of v3, /device:TPU:1, one launch (start us, length us, event | category | flops | bytes accessed | tf_op | source)
XLA Modules:
  0.0 271.8 jit_solution(15556459208905802191)
XLA Ops:
  0.7 0.8 and_select_fusion.1
  1.5 0.7 broadcast_in_dim.43
  2.2 0.7 broadcast_in_dim.47
  2.9 1.3 pad_add_fusion.meta_ref
  4.2 0.6 pad.18.gain_ref
  4.8 0.6 pad.17.gain_ref
  5.5 1.7 broadcast_in_dim.44.ids_ref
  7.1 0.9 slice_dynamic-update-slice_fusion.3
  8.0 0.9 slice_dynamic-update-slice_fusion.2
  8.9 0.9 slice_dynamic-update-slice_fusion.1
  9.8 0.9 slice_dynamic-update-slice_fusion
  10.8 1.0 constant_dynamic-update-slice_fusion
  11.7 1.0 bitcast_dynamic-update-slice_fusion.w_ref
  12.8 1.4 copy.25.tok_ref
  14.2 171.9 %front.1 = (bf16[1024,512]{1,0:T(8,128)(2,1)}, bf16[1024,512]{1,0:T(8,128)(2,1)}, bf16[4608,512]{1,0:T(8,128)(2,1)}, s32[16,16,128]{2,1,0:T(8,128)}) custom-call(bf16[1024,576]{1,0:T(8,128)(2,1)} %copy.25.tok_ref, bf16[288,1536]{1,0:T(8,128)(2,1)} %copy-done.2, s32[16,128]{1,0:T(8,128)} %pad_add_fusion.meta_ref, bf16[16,576]{1,0:T(8,128)(2,1)} %pad.17.gain_ref, ...), custom_call_target="tpu_custom_call" | custom-call | flops 18253611008 | bytes 33554432 | tf_op jit(solution)/shard_map/front/pallas_call | solution.py:459
  186.2 0.9 slice_reduce_fusion
  187.1 0.2 select_reduce_fusion
  187.3 1.5 reshape.114
  188.8 0.9 fusion.6
  189.8 2.6 copy.43
  192.3 74.5 %tail.1 = (bf16[1024,576]{1,0:T(8,128)(2,1)}, bf16[16,2,128,256]{3,2,1,0:T(8,128)(2,1)}) custom-call(bf16[1024,512]{1,0:T(8,128)(2,1)} %get-tuple-element.32.attn_ref, bf16[1024,576]{1,0:T(8,128)(2,1)} %copy.25.tok_ref, bf16[16,576]{1,0:T(8,128)(2,1)} %pad.18.gain_ref, bf16[4608,512]{1,0:T(8,128)(2,1)} %get-tuple-element.33.w_hbm, ...), custom_call_target="tpu_custom_call" | custom-call | flops 4831838208 | bytes 25165824 | tf_op jit(solution)/shard_map/tail/pallas_call | solution.py:678
  266.8 2.5 copy.30
  269.3 1.2 fusion.3
  270.6 1.2 copy.31
  (16 shorter events, 0.2 us)
Async XLA Ops:
  0.6 12.1 %copy-start.1 = (bf16[1024,576]{0,1:T(8,128)(2,1)S(1)}, bf16[1024,576]{0,1:T(8,128)(2,1)}, u32[]{:S(2)}) copy-start(bf16[1024,576]{0,1:T(8,128)(2,1)} %param.13) | copy-start | bytes 3538948
  2.9 11.3 %copy-start.3 = (f32[8,128]{1,0:T(8,128)}, f32[8,128]{1,0:T(8,128)S(1)}, u32[]{:S(2)}) copy-start(f32[8,128]{1,0:T(8,128)S(1)} %scatter.9.freq_ref) | copy-start | bytes 12292
  12.7 1.5 copy-start.2
  266.8 2.5 copy-start

commit v4 on v3

--- a/solution.py
+++ b/solution.py
@@ -32,7 +32,7 @@
 
 
 def front_kernel(
-    tok_ref, w_ref, meta_ref, gain_ref, ids_ref, freq_ref,
+    tok_ref, wq_ref, wk_ref, wv_ref, wo_ref, meta_ref, gain_ref, ids_ref, freq_ref,
     out_ref, kv_hbm, w_out_hbm, meta_out,
     tok, w, meta_all, gain_all, cos_ref, sin_ref, floor_ref, query_all, held, total,
     w_send, w_recv, z_send, z_recv, c_send, c_recv, m_send, m_recv, g_send, g_recv, own_sem,
@@ -42,9 +42,10 @@
     narrow = lax.axis_index("narrow")
     x, y = lax.div(wide, NY), lax.rem(wide, NY)
     z, core = lax.div(narrow, 2), lax.rem(narrow, 2)
-    shard = w_ref.shape[0]
-    part_rows = shard // 2
-    half = w_ref.shape[1] // WAVES
+    shard = wq_ref.shape[0]
+    part_rows = (shard * 7 // 18, shard - shard * 7 // 18)
+    part_first = (0, part_rows[0])
+    half = wq_ref.shape[1]
     parts, tokens, width = tok.shape
     blocks = tokens // QB
 
@@ -75,53 +76,59 @@
             block = ring(x, NX, along) * NY + ring(y, NY, across)
         else:
             block = ring(x, NX, across) * NY + ring(y, NY, along)
-        return pl.ds(pl.multiple_of(block * shard + part * part_rows, 16), part_rows)
-
-    sent = {}
-
-    def go(wave, part, group, kind, along, across, own=False):
+        return pl.ds(pl.multiple_of(block * shard + part_first[part], 16), part_rows[part])
+
+    def hop(wave, part, group, kind):
         where = peer(part, 0 if group == 0 else 1, 1 if kind % 2 == 0 else -1)
-        there = rows_of(part, along, across)
+        passed = (0, 0, -1, 1)[kind]
+        if group == 0:
+            there = rows_of(part, passed, 0)
+        else:
+            there = rows_of(part, (0, -1, 1, 2)[group - 1], passed)
         if kind < 2:
             span = pl.ds(wave * half, half)
         else:
             span = pl.ds(wave * half + (kind - 2) * (half // 2), half // 2)
-        src = w_ref.at[pl.ds(part * part_rows, part_rows), span] if own else w.at[there, span]
-        sent[wave, part, group, kind] = remote(
-            src, w.at[there, span],
-            w_send.at[wave, part, group, kind], w_recv.at[wave, part, group, kind], where,
-        )
+        return pltpu.make_async_remote_copy(
+            src_ref=w.at[there, span], dst_ref=w.at[there, span],
+            send_sem=w_send.at[wave, part, group, kind],
+            recv_sem=w_recv.at[wave, part, group, kind],
+            device_id=where, device_id_type=MESH,
+        )
+
+    def go(wave, part, group, kind):
+        hop(wave, part, group, kind).start()
 
     def got(wave, part, group, kind):
-        sent[wave, part, group, kind].wait_recv()
+        hop(wave, part, group, kind).wait_recv()
 
     def wave_own(wave):
         for group in (0, 1):
             for part in (0, 1):
-                go(wave, part, group, 0, 0, 0, True)
-                go(wave, part, group, 1, 0, 0, True)
+                go(wave, part, group, 0)
+                go(wave, part, group, 1)
 
     def wave_first(wave):
-        for kind, along, group in ((0, -1, 2), (1, 1, 3)):
+        for kind, group in ((0, 2), (1, 3)):
             for part in (0, 1):
                 got(wave, part, 0, kind)
-                go(wave, part, 0, 2 + kind, along, 0)
-                go(wave, part, group, 0, along, 0)
-                go(wave, part, group, 1, along, 0)
-
-    def wave_pass(wave, group, along):
+                go(wave, part, 0, 2 + kind)
+                go(wave, part, group, 0)
+                go(wave, part, group, 1)
+
+    def wave_pass(wave, group):
         for part in (0, 1):
             got(wave, part, group, 0)
-            go(wave, part, group, 2, along, -1)
+            go(wave, part, group, 2)
             got(wave, part, group, 1)
-            go(wave, part, group, 3, along, 1)
+            go(wave, part, group, 3)
 
     def wave_far(wave):
         for part in (0, 1):
             got(wave, part, 0, 2)
             got(wave, part, 0, 3)
-            go(wave, part, 4, 0, 2, 0)
-            go(wave, part, 4, 1, 2, 0)
+            go(wave, part, 4, 0)
+            go(wave, part, 4, 1)
 
     def wave_end(wave):
         for group in range(1, 5):
@@ -147,6 +154,20 @@
     def zblock(step):
         return ring(z, NZ, step) * 2 + core
 
+    own_rows = pl.ds(pl.multiple_of(wide * shard, 16), shard)
+    pieces = [(wq_ref, half), (wo_ref, 2 * half)]
+    for g in range(2):
+        there = slice(g * HD, (g + 1) * HD)
+        pieces.append((wk_ref.at[:, there], g * 256))
+        pieces.append((wv_ref.at[:, there], g * 256 + HD))
+    loads = [
+        pltpu.make_async_copy(
+            piece, w.at[own_rows, pl.ds(column, piece.shape[1])], own_sem.at[3 + i]
+        )
+        for i, (piece, column) in enumerate(pieces)
+    ]
+    for copy in loads[2:] + loads[:2]:
+        copy.start()
     small = []
     for other in range(1, NX * NY):
         target = lax.rem(wide + other, NX * NY)
@@ -156,18 +177,22 @@
         target = lax.rem(narrow + other, NZ * 2)
         small.append(remote(
             gain_ref, gain_all.at[narrow], g_send.at[other], g_recv.at[other], {"narrow": target}))
+    zgo(0, narrow, tok_ref.at[low], low)
+    zgo(1, narrow, tok_ref.at[high], high)
+    for copy in loads:
+        copy.wait()
     wave_own(0)
-    zgo(0, narrow, tok_ref, every)
-    zgo(1, narrow, tok_ref, every)
+    zgo(4, narrow, tok_ref.at[high], high)
+    zgo(5, narrow, tok_ref.at[low], low)
     cgo(0, narrow, tok_ref, every)
     local = [
-        pltpu.make_async_copy(w_ref, w.at[pl.ds(wide * shard, shard)], own_sem.at[0]),
-        pltpu.make_async_copy(tok_ref, tok.at[narrow], own_sem.at[1]),
-        pltpu.make_async_copy(meta_ref, meta_all.at[wide], own_sem.at[2]),
-        pltpu.make_async_copy(gain_ref, gain_all.at[narrow], own_sem.at[3]),
+        pltpu.make_async_copy(tok_ref, tok.at[narrow], own_sem.at[0]),
+        pltpu.make_async_copy(meta_ref, meta_all.at[wide], own_sem.at[1]),
+        pltpu.make_async_copy(gain_ref, gain_all.at[narrow], own_sem.at[2]),
     ]
     for copy in local:
         copy.start()
+    wave_own(1)
     wave_first(0)
 
     for copy in small:
@@ -196,32 +221,42 @@
         floor_ref[rows, :] = jnp.maximum(start, index - WINDOW + 1) - (first_token - WINDOW)
         return carry
 
-    wave_pass(0, 1, 0)
+    wave_pass(0, 1)
     wave_far(0)
     toks[0].wait_recv()
     zgo(2, zblock(-1), tok.at[zblock(-1), low], low)
-    cgo(1, zblock(-1), tok.at[zblock(-1)], every)
+    cgo(1, zblock(-1), tok.at[zblock(-1), low], low)
     toks[1].wait_recv()
     zgo(3, zblock(1), tok.at[zblock(1), high], high)
-    cgo(2, zblock(1), tok.at[zblock(1)], every)
-    wave_own(1)
+    cgo(2, zblock(1), tok.at[zblock(1), high], high)
+    wave_own(2)
     lax.fori_loop(0, blocks, tables, 0)
-    wave_pass(0, 2, -1)
-    wave_pass(0, 3, 1)
-    wave_pass(0, 4, 2)
+    wave_pass(0, 2)
+    wave_pass(0, 3)
+    wave_pass(0, 4)
     wave_first(1)
+    wave_pass(1, 1)
+    wave_far(1)
+    toks[4].wait_recv()
+    cgo(5, zblock(-1), tok.at[zblock(-1), high], high)
+    toks[5].wait_recv()
+    cgo(6, zblock(1), tok.at[zblock(1), low], low)
+    wave_pass(1, 2)
+    wave_pass(1, 3)
+    wave_pass(1, 4)
+    wave_first(2)
     toks[2].wait_recv()
     cgo(3, zblock(2), tok.at[zblock(2), low], low)
     toks[3].wait_recv()
     cgo(4, zblock(2), tok.at[zblock(2), high], high)
-    wave_pass(1, 1, 0)
-    wave_far(1)
     wave_end(0)
-    for kind in range(5):
+    wave_pass(2, 1)
+    wave_far(2)
+    for kind in range(7):
         pair[kind].wait_recv()
-    for kind in range(5):
+    for kind in range(7):
         pair[kind].wait_send()
-    for kind in range(4):
+    for kind in range(6):
         toks[kind].wait_send()
     done = [id(copy) for copy in list(pair.values()) + list(toks.values())]
     started[:] = [copy for copy in started if id(copy) not in done]
@@ -306,7 +341,7 @@
 
         return carry
 
-    def chunk(d, g, qb, first, size, diagonal=False, fresh=False):
+    def weigh(d, g, qb, first, size, diagonal=False):
         qrows = block_rows(qb)
         krows = pl.ds(pl.multiple_of(first, 256), size)
         query = jnp.concatenate(
@@ -333,7 +368,10 @@
             axis=0,
         )
         wide_values = jnp.concatenate([values, jnp.ones_like(values)], axis=1)
-        product = jnp.dot(weights, wide_values, preferred_element_type=jnp.float32)
+        return jnp.dot(weights, wide_values, preferred_element_type=jnp.float32)
+
+    def chunk(d, g, qb, first, size, diagonal=False, fresh=False):
+        product = weigh(d, g, qb, first, size, diagonal)
         slot = g * blocks + qb
         if fresh:
             total[slot] = product
@@ -348,71 +386,76 @@
 
     def segment(d, k, pairs):
         def pair(t, carry):
-            chunk(d, lax.rem(t, 2), lax.div(t, 2), k * QB, QB)
+            first = weigh(d, 0, t, k * QB, QB)
+            second = weigh(d, 1, t, k * QB, QB)
+            total[t] += first
+            total[blocks + t] += second
             return carry
 
         lax.fori_loop(0, pairs, pair, 0)
 
-    wave_own(2)
-    lax.fori_loop(0, 2, key_block, 0)
-    wave_pass(1, 2, -1)
-    wave_pass(1, 3, 1)
-    wave_pass(1, 4, 2)
-    wave_first(2)
-    lax.fori_loop(2, blocks, key_block, 0)
-    wave_pass(2, 1, 0)
-    wave_far(2)
+    for b in range(blocks):
+        lax.fori_loop(b, b + 1, key_block, 0)
+        lax.fori_loop(b, b + 1, begin, 0)
+        if b == 1:
+            wave_pass(2, 2)
+        if b == 2:
+            wave_pass(2, 3)
+    wave_pass(2, 4)
     save = pltpu.make_async_copy(held.at[0], kv_hbm, out_sem.at[0])
     save.start()
+
+    def pump(c):
+        along_x(c).wait_recv()
+
+        @pl.when(y == NY - 1)
+        def _():
+            up(4, c).start()
+
+        @pl.when(y > 0)
+        def _():
+            down(4, c).start()
+
     wave_end(1)
     lax.fori_loop(0, 2, query_block, 0)
-    wave_pass(2, 2, -1)
-    wave_pass(2, 3, 1)
+    pump(0)
     lax.fori_loop(2, blocks, query_block, 0)
-    wave_pass(2, 4, 2)
-    lax.fori_loop(0, blocks, begin, 0)
-    lax.fori_loop(0, 2 * blocks, own_pair, 0)
+    pump(1)
+    lax.fori_loop(0, blocks, own_pair, 0)
+    pump(2)
+    lax.fori_loop(blocks, 2 * blocks, own_pair, 0)
+    pump(3)
 
     def step(i, carry):
         @pl.when(i < blocks)
         def _():
-            along_x(i).wait_recv()
-
-            @pl.when(y == NY - 1)
-            def _():
-                up(4, i).start()
-
-            @pl.when(y > 0)
-            def _():
-                down(4, i).start()
-
             up(0, i).wait_recv()
 
             @pl.when(inner)
             def _():
                 pass_up(i).start()
 
-            segment(4, i, 2 * (i + 1))
-            segment(1, i, 2 * blocks)
-
-        @pl.when((i >= 1) & (i < blocks + 1))
-        def _():
-            down(0, i - 1).wait_recv()
+            segment(4, i, i + 1)
+            down(0, i).wait_recv()
 
             @pl.when(inner)
             def _():
-                pass_down(i - 1).start()
-
-            segment(3, i - 1, 2 * blocks)
-
-        @pl.when(i >= 2)
+                pass_down(i).start()
+
+            segment(1, i, blocks)
+
+        @pl.when(i < blocks)
         def _():
-            pass_up(i - 2).wait_recv()
-            segment(2, i - 2, 2 * blocks)
+            segment(3, i, blocks)
+
+        @pl.when(i >= 1)
+        def _():
+            pass_up(i - 1).wait_recv()
+            segment(2, i - 1, blocks)
 
         return carry
 
-    lax.fori_loop(0, blocks + 2, step, 0)
+    lax.fori_loop(0, blocks + 1, step, 0)
 
     def finish(t, carry):
         g, qb = lax.div(t, blocks), lax.rem(t, blocks)
@@ -444,13 +487,18 @@
     lax.fori_loop(0, blocks, drain, 0)
     for copy in started:
         copy.wait_send()
+    for wave in range(WAVES):
+        for part in (0, 1):
+            for group in range(5):
+                for kind in range(4):
+                    hop(wave, part, group, kind).wait_send()
     save_w.wait()
 
 
-def front(tokens, weights, meta, gain, ids, freq):
+def front(tokens, w_query, w_key, w_value, w_out_rows, meta, gain, ids, freq):
     rows, width = tokens.shape
-    shard, columns = weights.shape
-    half = columns // WAVES
+    shard, half = w_query.shape
+    columns = WAVES * half
     vmem_spec = pl.BlockSpec(memory_space=pltpu.VMEM)
     any_spec = pl.BlockSpec(memory_space=pl.ANY)
     dma = pltpu.SemaphoreType.DMA
@@ -464,7 +512,7 @@
             jax.ShapeDtypeStruct((16 * shard, half), bf16),
             jax.ShapeDtypeStruct((16,) + meta.shape, meta.dtype),
         ),
-        in_specs=[vmem_spec] * 6,
+        in_specs=[any_spec] * 5 + [vmem_spec] * 4,
         out_specs=(vmem_spec, any_spec, any_spec, any_spec),
         scratch_shapes=[
             pltpu.VMEM((8, rows, width), bf16),
@@ -477,8 +525,8 @@
             pltpu.VMEM((rows, half), bf16),
             pltpu.VMEM((REACH + 1, rows, half), bf16),
             pltpu.VMEM((8, 2 * QB, 256), jnp.float32),
-            dma((3, 2, 5, 4)), dma((3, 2, 5, 4)), dma((4,)), dma((4,)), dma((5,)), dma((5,)),
-            dma((16,)), dma((16,)), dma((8,)), dma((8,)), dma((4,)),
+            dma((3, 2, 5, 4)), dma((3, 2, 5, 4)), dma((6,)), dma((6,)), dma((7,)), dma((7,)),
+            dma((16,)), dma((16,)), dma((8,)), dma((8,)), dma((9,)),
             dma((3,)), dma((5, blocks)), dma((REACH + 1, blocks)),
         ],
         cost_estimate=pl.CostEstimate(
@@ -489,7 +537,7 @@
             vmem_limit_bytes=60 << 20, has_side_effects=True
         ),
         name="front",
-    )(tokens, weights, meta, gain, ids, freq)
+    )(tokens, w_query, w_key, w_value, w_out_rows, meta, gain, ids, freq)
 
 
 def tail_kernel(
@@ -715,20 +763,17 @@
     seg_rows = segment_ids.reshape(8, tok_w // 8)
     table_row = jnp.pad(page_table[None, :], ((0, 7), (0, tok_w // 8 - block_count)))
     meta = jnp.concatenate([seg_rows, table_row], axis=0)
-    gain_in = jnp.pad(pre_gain[None, :], ((0, 15), (0, 0)))
-    columns = []
-    for g in range(pairs_here):
-        columns += [w_key[:, g * HD : (g + 1) * HD], w_value[:, g * HD : (g + 1) * HD]]
-    weights = jnp.concatenate(columns + [w_query, jnp.transpose(w_out)], axis=1)
+    gain_in = jnp.broadcast_to(pre_gain[None, :], (16, pre_gain.shape[0]))
     half_width = HD // 2
     inverse_freq = jnp.exp(
-        -math.log(10000.0) * 2.0 * jnp.arange(half_width, dtype=jnp.float32) / HD
+        -math.log(10000.0) * 2.0 * (jnp.arange(HD) % half_width).astype(jnp.float32) / HD
     )
     signs = jnp.where(jnp.arange(HD) < half_width, -1.0, 1.0)
-    freq = jnp.zeros((8, HD), jnp.float32)
-    freq = freq.at[0].set(jnp.concatenate([inverse_freq, inverse_freq])).at[1].set(signs)
+    freq = jnp.where(jnp.arange(8)[:, None] == 0, inverse_freq[None, :], signs[None, :])
     ids = jnp.broadcast_to(segment_ids[:, None], (tok_w, 128))
-    attn_out, flat, w_all, meta_all = front(tokens, weights, meta, gain_in, ids, freq)
+    attn_out, flat, w_all, meta_all = front(
+        tokens, w_query, w_key, w_value, jnp.transpose(w_out), meta, gain_in, ids, freq
+    )
     table_all = meta_all[:, 8, :block_count].reshape(-1)
 
     page_len = tok_w // block_count
@@ -740,7 +785,7 @@
         "sj,jpgc->sgpc", send_pick, token_blocks, preferred_element_type=jnp.float32
     ).astype(jnp.bfloat16)
     mixed, incoming = tail(
-        attn_out, w_all, tokens, jnp.pad(post_gain[None, :], ((0, 15), (0, 0))), outgoing
+        attn_out, w_all, tokens, post_gain[None, :], outgoing
     )
     my_pages = shard_index * block_count + jnp.arange(block_count, dtype=jnp.int32)
     found_page = table_all[None, :] == my_pages[:, None]

time: 272 us -> 256 us (0.941)
  Pallas kernels: 246 us -> 235 us
  local copies, waits for them, and re-layouts: 20.1 us -> 15.2 us
    pallas_call x1, Pallas kernels: 172 us -> 159 us  [front(): pl.pallas_call(front_kernel, out_shape=(jax.ShapeDtypeStruct((rows, half)...]
    unnamed x16 -> x5, local copies, waits for them, and re-layouts: 9.8 us -> 6.15 us
where the time goes in v4:
time: 256 us
  Pallas kernels  235 us (92%)
  local copies, waits for them, and re-layouts  15.2 us (6%)
  other arithmetic  2.82 us (1%)
    pallas_call x1, Pallas kernels, front(): pl.pallas_call(front_kernel, out_shape=(jax.ShapeDtypeStruct((rows, half)...  159 us
    pallas_call x1, Pallas kernels, tail(): pl.pallas_call(tail_kernel, out_shape=(jax.ShapeDtypeStruct(tokens.shape,...  75.6 us
    unnamed x5, local copies, waits for them, and re-layouts  6.15 us

profile of v4, /device:TPU:1, one launch (start us, length us, event | category | flops | bytes accessed | tf_op | source)
XLA Modules:
  0.0 255.7 jit_solution(9275416477666575229)
XLA Ops:
  0.6 0.7 and_select_fusion.1
  1.3 0.7 broadcast_select_fusion.freq_ref
  2.0 1.3 broadcast_in_dim.79.gain_ref
  3.3 1.3 pad_add_fusion.meta_ref
  4.6 1.3 broadcast_in_dim.72.gain_ref
  5.9 1.7 broadcast_in_dim.73.ids_ref
  7.5 2.4 copy.25.tok_ref
  9.9 159.1 %front.1 = (bf16[1024,512]{1,0:T(8,128)(2,1)}, bf16[1024,512]{1,0:T(8,128)(2,1)}, bf16[4608,512]{1,0:T(8,128)(2,1)}, s32[16,16,128]{2,1,0:T(8,128)}) custom-call(bf16[1024,576]{1,0:T(8,128)(2,1)} %copy.25.tok_ref, bf16[288,512]{1,0:T(8,128)(2,1)} %wq_ref.1, bf16[288,256]{1,0:T(8,128)(2,1)} %wk_ref.1, bf16[288,256]{1,0:T(8,128)(2,1)} %wv_ref.1, ...), custom_call_target="tpu_custom_call" | custom-call | flops 18253611008 | bytes 33554432 | tf_op jit(solution)/shard_map/front/pallas_call | solution.py:507
  169.1 0.9 slice_reduce_fusion
  170.0 0.1 eq.55
  170.0 0.2 select_reduce_fusion
  170.2 1.3 reshape.79
  171.6 0.9 fusion.6
  172.5 2.6 %copy.43 = bf16[128,2,256,16]{2,0,1,3:T(8,128)(2,1)} copy(bf16[128,2,256,16]{2,3,1,0:T(8,128)(2,1)S(1)} %fusion.6) | data formatting | bytes 4194304 | tf_op jit(solution)/shard_map/sj,jpgc->sgpc/dot_general | solution.py:784
  175.1 75.6 %tail.1 = (bf16[1024,576]{1,0:T(8,128)(2,1)}, bf16[16,2,128,256]{3,2,1,0:T(8,128)(2,1)}) custom-call(bf16[1024,512]{1,0:T(8,128)(2,1)} %get-tuple-element.8.attn_ref, bf16[1024,576]{1,0:T(8,128)(2,1)} %copy.25.tok_ref, bf16[1,576]{1,0:T(2,128)(2,1)} %broadcast_in_dim.79.gain_ref, bf16[4608,512]{1,0:T(8,128)(2,1)} %get-tuple-element.9.w_hbm, ...), custom_call_target="tpu_custom_call" | custom-call | flops 4831838208 | bytes 25165824 | tf_op jit(solution)/shard_map/tail/pallas_call | solution.py:726
  250.7 0.0 copy-start
  250.7 2.5 copy.30
  253.3 0.0 copy-done
  253.3 1.2 fusion.3
  254.5 1.2 copy.31
  (4 shorter events, 0.0 us)
Async XLA Ops:
  250.7 2.5 copy-start

commit v5 on v4

--- a/solution.py
+++ b/solution.py
@@ -1,8 +1,8 @@
-import functools
 import math
 
 import jax
 import jax.numpy as jnp
+import numpy as np
 from jax import lax
 from jax.experimental import pallas as pl
 from jax.experimental.pallas import tpu as pltpu
@@ -602,15 +602,17 @@
 
         lax.fori_loop(0, size // QB, step, 0)
 
-    passes = []
-    for i in range(4):
-        loads[i].wait()
-
-        def fill(rows, i=i):
+    passes = {}
+
+    def hand_over(i, part):
+        def fill(rows):
             give[i, rows, :] = term(i, rows)
 
-        over_rows(fill)
-        passes.append(remote(give.at[i], take.at[i], c_send.at[i], c_recv.at[i], sibling))
+        over_rows(fill, part * mid, mid)
+        span = pl.ds(part * mid, mid)
+        passes[i, part] = remote(
+            give.at[i, span], take.at[i, span], c_send.at[i, part], c_recv.at[i, part], sibling
+        )
 
     def own_sum(i, rows):
         mine = term(4 + i, rows)
@@ -623,19 +625,32 @@
         return body
 
     ahead, behind = {"narrow": at_z(1) * 2 + core}, {"narrow": at_z(-1) * 2 + core}
-    for i in range(4, 8):
-        loads[i].wait()
-    passes[0].wait_recv()
+    loads[0].wait()
+    hand_over(0, 0)
+    hand_over(0, 1)
+    loads[1].wait()
+    hand_over(1, 1)
+    loads[4].wait()
+    passes[0, 0].wait_recv()
     over_rows(put(0), 0, mid)
     far_up = remote(stage.at[0, low], far.at[0], f_send.at[0], f_recv.at[0], ahead)
+    passes[0, 1].wait_recv()
     over_rows(put(0), mid, mid)
     far_down = remote(stage.at[0, high], far.at[1], f_send.at[1], f_recv.at[1], behind)
-    passes[1].wait_recv()
+    loads[2].wait()
+    hand_over(2, 0)
+    loads[5].wait()
+    passes[1, 1].wait_recv()
     over_rows(put(1), mid, mid)
     near_a = remote(stage.at[1, high], near.at[0, high], n_send.at[0], n_recv.at[0], ahead)
-    passes[2].wait_recv()
+    loads[6].wait()
+    passes[2, 0].wait_recv()
     over_rows(put(2), 0, mid)
     near_b = remote(stage.at[2, low], near.at[1, low], n_send.at[1], n_recv.at[1], behind)
+    hand_over(1, 0)
+    hand_over(2, 1)
+    passes[1, 0].wait_recv()
+    passes[2, 1].wait_recv()
 
     far_up.wait_recv()
 
@@ -658,7 +673,12 @@
 
     lax.fori_loop(0, mid // QB, with_far_down, 0)
     near_d = remote(stage.at[2, high], near.at[1, high], n_send.at[3], n_recv.at[3], behind)
-    passes[3].wait_recv()
+    loads[3].wait()
+    loads[7].wait()
+    hand_over(3, 0)
+    hand_over(3, 1)
+    passes[3, 0].wait_recv()
+    passes[3, 1].wait_recv()
 
     def keep(rows):
         kept[rows, :] = own_sum(3, rows)
@@ -711,7 +731,7 @@
     for copy in pages:
         copy.wait_recv()
     own.wait()
-    for copy in pages + passes + sums:
+    for copy in pages + list(passes.values()) + sums:
         copy.wait_send()
     for copy in (far_up, far_down, near_a, near_b, near_c, near_d):
         copy.wait_send()
@@ -741,7 +761,7 @@
             pltpu.VMEM((2, rows, width), bf16),
             pltpu.VMEM((rows, width), jnp.float32),
             pltpu.VMEM((8, 8, rows), jnp.float32),
-            dma((16,)), dma((16,)), dma, dma((4,)), dma((4,)), dma((2,)), dma((2,)),
+            dma((16,)), dma((16,)), dma, dma((4, 2)), dma((4, 2)), dma((2,)), dma((2,)),
             dma((4,)), dma((4,)), dma((8,)), dma((8,)),
         ],
         cost_estimate=pl.CostEstimate(
@@ -765,11 +785,10 @@
     meta = jnp.concatenate([seg_rows, table_row], axis=0)
     gain_in = jnp.broadcast_to(pre_gain[None, :], (16, pre_gain.shape[0]))
     half_width = HD // 2
-    inverse_freq = jnp.exp(
-        -math.log(10000.0) * 2.0 * (jnp.arange(HD) % half_width).astype(jnp.float32) / HD
-    )
-    signs = jnp.where(jnp.arange(HD) < half_width, -1.0, 1.0)
-    freq = jnp.where(jnp.arange(8)[:, None] == 0, inverse_freq[None, :], signs[None, :])
+    lane = np.arange(HD)
+    inverse_freq = np.exp(-math.log(10000.0) * 2.0 * (lane % half_width) / HD)
+    signs = np.where(lane < half_width, -1.0, 1.0)
+    freq = jnp.asarray(np.stack([inverse_freq] + [signs] * 7).astype(np.float32))
     ids = jnp.broadcast_to(segment_ids[:, None], (tok_w, 128))
     attn_out, flat, w_all, meta_all = front(
         tokens, w_query, w_key, w_value, jnp.transpose(w_out), meta, gain_in, ids, freq

time: 256 us -> 252 us (0.984)
  Pallas kernels: 235 us -> 231 us
    pallas_call x1, Pallas kernels: 75.6 us -> 72.3 us  [tail(): pl.pallas_call(tail_kernel, out_shape=(jax.ShapeDtypeStruct(tokens.shape,...]
where the time goes in v5:
time: 252 us
  Pallas kernels  231 us (92%)
  local copies, waits for them, and re-layouts  15.3 us (6%)
    pallas_call x1, Pallas kernels, front(): pl.pallas_call(front_kernel, out_shape=(jax.ShapeDtypeStruct((rows, half)...  159 us
    pallas_call x1, Pallas kernels, tail(): pl.pallas_call(tail_kernel, out_shape=(jax.ShapeDtypeStruct(tokens.shape,...  72.3 us
    unnamed x5, local copies, waits for them, and re-layouts  6.15 us

profile of v5, /device:TPU:1, one launch (start us, length us, event | category | flops | bytes accessed | tf_op | source)
XLA Modules:
  0.0 251.7 jit_solution(9098737346005963723)
XLA Ops:
  0.6 0.7 and_select_fusion.1
  1.3 1.3 broadcast_in_dim.23.gain_ref
  2.6 1.3 pad_add_fusion.meta_ref
  3.9 1.3 broadcast_in_dim.17.gain_ref
  5.2 1.7 broadcast_in_dim.22.ids_ref
  6.9 2.4 copy.26.tok_ref
  9.3 159.1 %front.1 = (bf16[1024,512]{1,0:T(8,128)(2,1)}, bf16[1024,512]{1,0:T(8,128)(2,1)}, bf16[4608,512]{1,0:T(8,128)(2,1)}, s32[16,16,128]{2,1,0:T(8,128)}) custom-call(bf16[1024,576]{1,0:T(8,128)(2,1)} %copy.26.tok_ref, bf16[288,512]{1,0:T(8,128)(2,1)} %wq_ref.1, bf16[288,256]{1,0:T(8,128)(2,1)} %wk_ref.1, bf16[288,256]{1,0:T(8,128)(2,1)} %wv_ref.1, ...), custom_call_target="tpu_custom_call" | custom-call | flops 18253611008 | bytes 33554432 | tf_op jit(solution)/shard_map/front/pallas_call | solution.py:507
  168.4 0.9 slice_reduce_fusion
  169.3 0.1 eq.44
  169.4 0.2 select_reduce_fusion
  169.5 1.3 reshape.57
  170.9 0.9 fusion.6
  171.8 2.6 %copy.44 = bf16[128,2,256,16]{2,0,1,3:T(8,128)(2,1)} copy(bf16[128,2,256,16]{2,3,1,0:T(8,128)(2,1)S(1)} %fusion.6) | data formatting | bytes 4194304 | tf_op jit(solution)/shard_map/sj,jpgc->sgpc/dot_general | solution.py:803
  174.4 72.3 %tail.1 = (bf16[1024,576]{1,0:T(8,128)(2,1)}, bf16[16,2,128,256]{3,2,1,0:T(8,128)(2,1)}) custom-call(bf16[1024,512]{1,0:T(8,128)(2,1)} %get-tuple-element.8.attn_ref, bf16[1024,576]{1,0:T(8,128)(2,1)} %copy.26.tok_ref, bf16[1,576]{1,0:T(2,128)(2,1)} %broadcast_in_dim.23.gain_ref, bf16[4608,512]{1,0:T(8,128)(2,1)} %get-tuple-element.9.w_hbm, ...), custom_call_target="tpu_custom_call" | custom-call | flops 4831838208 | bytes 25165824 | tf_op jit(solution)/shard_map/tail/pallas_call | solution.py:746
  246.7 0.0 copy-start
  246.7 2.5 %copy.31 = bf16[1024,576]{0,1:T(8,128)(2,1)} copy(bf16[1024,576]{1,0:T(8,128)(2,1)} %get-tuple-element.18) | data formatting | bytes 2359296
  249.3 0.0 copy-done
  249.3 1.2 fusion.3
  250.5 1.2 copy.32
  (2 shorter events, 0.0 us)
Async XLA Ops:
  246.7 2.5 %copy-start = (bf16[16,2,128,256]{3,2,1,0:T(8,128)(2,1)S(1)}, bf16[16,2,128,256]{3,2,1,0:T(8,128)(2,1)}, u32[]{:S(2)}) copy-start(bf16[16,2,128,256]{3,2,1,0:T(8,128)(2,1)} %get-tuple-element.13) | copy-start | bytes 6291460

commit v6 on v5

--- a/solution.py
+++ b/solution.py
@@ -402,8 +402,13 @@
         if b == 2:
             wave_pass(2, 3)
     wave_pass(2, 4)
-    save = pltpu.make_async_copy(held.at[0], kv_hbm, out_sem.at[0])
-    save.start()
+    saves = []
+    for j in range(kv_hbm.shape[0]):
+        for g in range(2):
+            saves.append(pltpu.make_async_copy(
+                held.at[0, pl.ds(j * 128, 128), pl.ds(g * 256, 256)], kv_hbm.at[j, g],
+                out_sem.at[3 + 2 * j + g]))
+            saves[-1].start()
 
     def pump(c):
         along_x(c).wait_recv()
@@ -469,7 +474,8 @@
     wave_end(2)
     save_w = pltpu.make_async_copy(w.at[:, pl.ds(2 * half, half)], w_out_hbm, out_sem.at[1])
     save_w.start()
-    save.wait()
+    for save in saves:
+        save.wait()
     save_meta.wait()
 
     def drain(c, carry):
@@ -508,7 +514,7 @@
         front_kernel,
         out_shape=(
             jax.ShapeDtypeStruct((rows, half), bf16),
-            jax.ShapeDtypeStruct((rows, half), bf16),
+            jax.ShapeDtypeStruct((rows // 128, 2, 128, 256), bf16),
             jax.ShapeDtypeStruct((16 * shard, half), bf16),
             jax.ShapeDtypeStruct((16,) + meta.shape, meta.dtype),
         ),
@@ -527,7 +533,7 @@
             pltpu.VMEM((8, 2 * QB, 256), jnp.float32),
             dma((3, 2, 5, 4)), dma((3, 2, 5, 4)), dma((6,)), dma((6,)), dma((7,)), dma((7,)),
             dma((16,)), dma((16,)), dma((8,)), dma((8,)), dma((9,)),
-            dma((3,)), dma((5, blocks)), dma((REACH + 1, blocks)),
+            dma((3 + rows // 64,)), dma((5, blocks)), dma((REACH + 1, blocks)),
         ],
         cost_estimate=pl.CostEstimate(
             flops=4 * rows * 4352 * 128 * 8, bytes_accessed=32 << 20,
@@ -779,7 +785,6 @@
     shard_count = lax.axis_size("wide")
     shard_index = lax.axis_index("wide")
     block_count = page_table.shape[0]
-    pairs_here = w_key.shape[1] // HD
     seg_rows = segment_ids.reshape(8, tok_w // 8)
     table_row = jnp.pad(page_table[None, :], ((0, 7), (0, tok_w // 8 - block_count)))
     meta = jnp.concatenate([seg_rows, table_row], axis=0)
@@ -795,13 +800,11 @@
     )
     table_all = meta_all[:, 8, :block_count].reshape(-1)
 
-    page_len = tok_w // block_count
-    token_blocks = flat.reshape(block_count, page_len, pairs_here, 2 * HD)
     owners = page_table // block_count
     shard_ids = jnp.arange(shard_count, dtype=jnp.int32)
     send_pick = (owners[None, :] == shard_ids[:, None]).astype(jnp.bfloat16)
     outgoing = jnp.einsum(
-        "sj,jpgc->sgpc", send_pick, token_blocks, preferred_element_type=jnp.float32
+        "sj,jgpc->sgpc", send_pick, flat, preferred_element_type=jnp.float32
     ).astype(jnp.bfloat16)
     mixed, incoming = tail(
         attn_out, w_all, tokens, post_gain[None, :], outgoing

time: 252 us -> 252 us (level)
  no operation moved by 1% of the time
where the time goes in v6:
time: 252 us; the launch traced here: 251 us
  Pallas kernels  232 us (92%)
  local copies, waits for them, and re-layouts  13.4 us (5%)
  matrix products  3.38 us (1%)
    pallas_call x1, Pallas kernels, front(): pl.pallas_call(front_kernel, out_shape=(jax.ShapeDtypeStruct((rows, half)...  159 us
    pallas_call x1, Pallas kernels, tail(): pl.pallas_call(tail_kernel, out_shape=(jax.ShapeDtypeStruct(tokens.shape,...  72.3 us
    unnamed x5, local copies, waits for them, and re-layouts  6.15 us

profile of v6, /device:TPU:1, one launch (start us, length us, event | category | flops | bytes accessed | tf_op | source)
XLA Modules:
  0.0 251.2 jit_solution(2930433831874902946)
XLA Ops:
  0.6 0.7 and_select_fusion.1
  1.3 1.3 broadcast_in_dim.23.gain_ref
  2.6 1.3 pad_add_fusion.meta_ref
  3.9 1.3 broadcast_in_dim.17.gain_ref
  5.2 1.7 broadcast_in_dim.22.ids_ref
  6.9 2.4 copy.26.tok_ref
  9.3 159.3 %front.1 = (bf16[1024,512]{1,0:T(8,128)(2,1)}, bf16[8,2,128,256]{3,2,1,0:T(8,128)(2,1)}, bf16[4608,512]{1,0:T(8,128)(2,1)}, s32[16,16,128]{2,1,0:T(8,128)}) custom-call(bf16[1024,576]{1,0:T(8,128)(2,1)} %copy.26.tok_ref, bf16[288,512]{1,0:T(8,128)(2,1)} %wq_ref.1, bf16[288,256]{1,0:T(8,128)(2,1)} %wk_ref.1, bf16[288,256]{1,0:T(8,128)(2,1)} %wv_ref.1, ...), custom_call_target="tpu_custom_call" | custom-call | flops 18253611008 | bytes 33554432 | tf_op jit(solution)/shard_map/front/pallas_call | solution.py:513
  168.6 0.9 slice_reduce_fusion
  169.4 0.1 eq.44
  169.5 0.2 select_reduce_fusion
  169.7 2.1 fusion.5
  171.8 2.1 copy.42.pages_hbm
  173.9 72.3 %tail.1 = (bf16[1024,576]{1,0:T(8,128)(2,1)}, bf16[16,2,128,256]{3,2,1,0:T(8,128)(2,1)}) custom-call(bf16[1024,512]{1,0:T(8,128)(2,1)} %get-tuple-element.8.attn_ref, bf16[1024,576]{1,0:T(8,128)(2,1)} %copy.26.tok_ref, bf16[1,576]{1,0:T(2,128)(2,1)} %broadcast_in_dim.23.gain_ref, bf16[4608,512]{1,0:T(8,128)(2,1)} %get-tuple-element.9.w_hbm, ...), custom_call_target="tpu_custom_call" | custom-call | flops 4831838208 | bytes 25165824 | tf_op jit(solution)/shard_map/tail/pallas_call | solution.py:752
  246.2 0.0 copy-start
  246.2 2.5 %copy.31 = bf16[1024,576]{0,1:T(8,128)(2,1)} copy(bf16[1024,576]{1,0:T(8,128)(2,1)} %get-tuple-element.18) | data formatting | bytes 2359296
  248.8 0.0 copy-done
  248.8 1.2 fusion.2
  250.0 1.2 copy.32
  (2 shorter events, 0.0 us)
Async XLA Ops:
  246.2 2.5 %copy-start = (bf16[16,2,128,256]{3,2,1,0:T(8,128)(2,1)S(1)}, bf16[16,2,128,256]{3,2,1,0:T(8,128)(2,1)}, u32[]{:S(2)}) copy-start(bf16[16,2,128,256]{3,2,1,0:T(8,128)(2,1)} %get-tuple-element.13) | copy-start | bytes 6291460
